TPU v7x, 256 devices: a whole 4x4x8 slice. The times are simulated.
256 devices in a mesh: cube: 4 (over y), grid: 64 (over z, x, core).
Axes of the slice: x: 4, y: 4, z: 8, core: 2. Of those that a mesh axis runs over, the one named last changes fastest.
Arguments:
- root_inverse: float32 [4096, 4096], P('grid', 'cube'), may hold values from -0.09375 to 0.09375
- level_inverse: float32 [1024, 2048], P('grid', 'cube'), may hold values from -0.1875 to 0.1875
- coupling: float32 [4096, 2048], P('grid', 'cube'), may hold values from -0.1875 to 0.1875
- pattern: int32 [2, 32], replicated, may hold values 0 or 1
Outputs:
- root_cov: float32 [4096, 4096], P('grid', 'cube')
- cross_cov: float32 [4096, 2048], P('grid', 'cube')
- node_cov: float32 [1024, 2048], P('grid', 'cube')
All inputs are finite; a program needn't handle non-finite values.
Results may differ from a plain program's by a relative error of at most 0.0001.
Values sent between devices are 32-bit elements; how exact they have to be, the bound alone decides.
No kernel may reach another device: no remote copies, remote signals or barrier semaphores. Data moves between devices by JAX's collectives and lax.ppermute only.
A program may use at most 128 MiB of HBM per device.

v0:
```python
import jax
import jax.numpy as jnp
from jax import lax
from jax.sharding import PartitionSpec as P

BLK = 128


HIGHEST = lax.Precision.HIGHEST


def from_partner(value, axis, apart):
    return lax.ppermute(value, axis, [(i, i ^ 1 << apart) for i in range(lax.axis_size(axis))])


def product(left, right):
    return jnp.dot(left, right, precision=HIGHEST, preferred_element_type=jnp.float32)


def lower_piece(weights, row_start, col_start):
    rows = row_start + lax.broadcasted_iota(jnp.int32, weights.shape, 0)
    cols = col_start + lax.broadcasted_iota(jnp.int32, weights.shape, 1)
    below = jnp.where(cols < rows, weights, jnp.zeros_like(weights))
    return below + jnp.where(cols == rows, 1.0, 0.0).astype(jnp.float32)


def join_halves(own, other, half):
    first = jnp.concatenate([own, other], axis=1)
    second = jnp.concatenate([other, own], axis=1)
    return jnp.where(half == 0, first, second)


def on_device(root_inverse, level_inverse, coupling, pattern):
    grid_index = lax.axis_index("grid")
    cube_index = lax.axis_index("cube")
    node = cube_index // 2
    half = cube_index % 2
    root_rows_dev, root_cols_dev = root_inverse.shape
    node_rows_dev, half_width = level_inverse.shape
    root_lower = lower_piece(root_inverse, grid_index * root_rows_dev, cube_index * root_cols_dev)
    node_lower = lower_piece(level_inverse, grid_index * node_rows_dev, half * half_width)
    row_ids = grid_index * root_rows_dev + jnp.arange(root_rows_dev, dtype=jnp.int32)
    block_count = pattern.shape[1]
    chosen = jnp.where(node == 0, pattern[0], pattern[1]).astype(jnp.float32)
    onehot = (
        jnp.arange(block_count, dtype=jnp.int32)[None, :] == (row_ids // BLK)[:, None]
    ).astype(jnp.float32)
    row_mask = jnp.sum(onehot * chosen[None, :], axis=1)[:, None]
    masked_coupling = coupling * row_mask
    lower_rows = lax.all_gather(root_lower, "cube", axis=1, tiled=True)
    root_cov = lax.psum_scatter(
        product(lower_rows.T, root_lower), "grid", scatter_dimension=0, tiled=True
    )
    cov_rows = lax.all_gather(root_cov, "cube", axis=1, tiled=True)
    other_coupling, other_lower = from_partner((masked_coupling, node_lower), "cube", 0)
    coupling_full = join_halves(masked_coupling, other_coupling, half)
    lower_full = join_halves(node_lower, other_lower, half)
    factor = product(coupling_full, lax.all_gather(node_lower, "grid", axis=0, tiled=True))
    cross = lax.psum_scatter(-product(cov_rows.T, factor), "grid", scatter_dimension=0, tiled=True)
    cross = cross * row_mask
    other_cross = from_partner(cross, "cube", 0)
    left_rows = join_halves(cross, other_cross, half)
    first = product(lower_full.T, node_lower)
    node_cov = lax.psum_scatter(
        first - product(left_rows.T, factor), "grid", scatter_dimension=0, tiled=True
    )
    return (root_cov, cross, node_cov)


def solution(mesh):
    placed = (P("grid", "cube"), P("grid", "cube"), P("grid", "cube"), P())
    return jax.shard_map(
        on_device,
        mesh=mesh,
        in_specs=placed,
        out_specs=(P("grid", "cube"), P("grid", "cube"), P("grid", "cube")),
        check_vma=False,
    )
```

profile of v0, /device:TPU:8, one launch (start us, length us, event | category | flops | bytes accessed | tf_op | source)
XLA Modules:
  0.0 671.0 jit_solution(15860373816275779728)
XLA Ops:
  7.2 1.8 select_add_fusion
  9.0 0.0 reduce-scatter.4.cloned.1.call-start
  9.1 29.8 %all-gather.4.cloned.1.call-done = f32[64,4096]{1,0:T(8,128)} async-done(((f32[64,1024]{1,0:T(8,128)}), f32[64,4096]{1,0:T(8,128)}) %all-gather.4.cloned.1.call-update) | async-done | bytes 1048592 | tf_op jit(solution)/shard_map/all_gather | solution.py:50
  38.9 16.9 %fusion.25 = f32[4096,1024]{1,0:T(8,128)} fusion(f32[64,4096]{1,0:T(8,128)} %all-gather.4.cloned.1.call-done, f32[64,1024]{1,0:T(8,128)} %select_add_fusion), kind=kOutput, calls=%fused_computation.45 | convolution fusion | flops 3221225472 | bytes 18087936 | tf_op jit(solution)/shard_map/dot_general | solution.py:17
  55.8 0.0 all-gather.8.cloned.1.call-start
  55.9 0.6 copy-done.3
  56.6 0.7 select_add_fusion.1
  57.3 189.2 %reduce-scatter.4.cloned.1.call-done = f32[64,1024]{1,0:T(8,128)} async-done(((f32[4096,1024]{1,0:T(8,128)}), f32[64,1024]{1,0:T(8,128)}) %reduce-scatter.4.cloned.1.call-update) | async-done | bytes 262160 | tf_op jit(solution)/shard_map/reduce_scatter | solution.py:51
  246.7 0.1 select_reduce_fusion
  246.8 0.1 broadcast_multiply_fusion.1
  246.9 0.6 collective-permute-start
  247.4 4.5 collective-permute-done
  251.9 73.5 %all-gather.8.cloned.1.call-done = f32[1024,512]{1,0:T(8,128)} async-done(((f32[16,512]{1,0:T(8,128)}), f32[1024,512]{1,0:T(8,128)}) %all-gather.8.cloned.1.call-update) | async-done | bytes 2097168 | tf_op jit(solution)/shard_map/all_gather | solution.py:58
  325.5 3.0 fusion
  328.4 22.7 %all-gather.6.cloned.1.call-done = f32[64,4096]{1,0:T(8,128)} async-done(((f32[64,1024]{1,0:T(8,128)}), f32[64,4096]{1,0:T(8,128)}) %all-gather.6.cloned.1.call-update) | async-done | bytes 1048592 | tf_op jit(solution)/shard_map/all_gather | solution.py:54
  351.1 10.0 %convolution_negate_fusion = f32[4096,512]{1,0:T(8,128)} fusion(f32[64,4096]{1,0:T(8,128)} %all-gather.6.cloned.1.call-done, f32[64,512]{1,0:T(8,128)S(1)} %fusion), kind=kOutput, calls=%fused_computation | convolution fusion | flops 1612709888 | bytes 9568256 | tf_op jit(solution)/shard_map/dot_general | solution.py:17
  361.2 152.8 %reduce-scatter.6.cloned.1.call-done = f32[64,512]{1,0:T(8,128)} async-done(((f32[4096,512]{1,0:T(8,128)}), f32[64,512]{1,0:T(8,128)}) %reduce-scatter.6.cloned.1.call-update) | async-done | bytes 131088 | tf_op jit(solution)/shard_map/reduce_scatter | solution.py:59
  514.0 1.0 broadcast_multiply_fusion
  514.9 0.6 collective-permute-start.2
  515.6 1.5 collective-permute-start.1
  517.1 2.9 collective-permute-done.2
  520.0 1.8 fusion.6
  521.9 3.2 convolution_subtract_fusion
  525.1 139.1 %reduce-scatter.8.cloned.1.call-done = f32[16,512]{1,0:T(8,128)} async-done(((f32[1024,512]{1,0:T(8,128)}), f32[16,512]{1,0:T(8,128)}) %reduce-scatter.8.cloned.1.call-update) | async-done | bytes 32784 | tf_op jit(solution)/shard_map/reduce_scatter | solution.py:64
  (26 shorter events, 0.3 us)
Async XLA Ops:
  7.2 31.7 %all-gather.4.cloned.1.call-start = ((), (), s32[]{:S(2)}) async-start(), calls=%async_computation.3 | async-start | bytes 1310720 | tf_op jit(solution)/shard_map/all_gather | solution.py:50
  9.0 237.5 %reduce-scatter.4.cloned.1.call-start = ((), (), s32[]{:S(2)}) async-start(), calls=%async_computation.4 | async-start | bytes 17039360 | tf_op jit(solution)/shard_map/reduce_scatter | solution.py:51
  55.8 0.8 copy-start.3
  55.8 190.9 %copy-start.4 = (s32[2,32]{1,0:T(2,128)S(1)}, s32[2,32]{1,0:T(2,128)}, u32[]{:S(2)}) copy-start(s32[2,32]{1,0:T(2,128)} %param.7) | copy-start | bytes 772
  55.8 191.0 %copy-start.2 = (f32[64,512]{1,0:T(8,128)S(1)}, f32[64,512]{1,0:T(8,128)}, u32[]{:S(2)}) copy-start(f32[64,512]{1,0:T(8,128)} %param.6) | copy-start | bytes 393220
  55.8 269.6 %all-gather.8.cloned.1.call-start = ((), (), s32[]{:S(2)}) async-start(), calls=%async_computation.6 | async-start | bytes 2129920 | tf_op jit(solution)/shard_map/all_gather | solution.py:58
  57.3 293.8 %all-gather.6.cloned.1.call-start = ((), (), s32[]{:S(2)}) async-start(), calls=%async_computation.5 | async-start | bytes 1310720 | tf_op jit(solution)/shard_map/all_gather | solution.py:54
  246.6 267.4 %reduce-scatter.6.cloned.1.call-start = ((), (), s32[]{:S(2)}) async-start(), calls=%async_computation.7 | async-start | bytes 8519680 | tf_op jit(solution)/shard_map/reduce_scatter | solution.py:59
  246.9 5.1 collective-permute-start
  361.1 154.5 %copy-start.1 = (f32[16,512]{1,0:T(8,128)S(1)}, f32[16,512]{1,0:T(8,128)}, u32[]{:S(2)}) copy-start(f32[16,512]{1,0:T(8,128)} %select_add_fusion.1) | copy-start | bytes 98308
  361.1 303.0 %reduce-scatter.8.cloned.1.call-start = ((), (), s32[]{:S(2)}) async-start(), calls=%async_computation.8 | async-start | bytes 2129920 | tf_op jit(solution)/shard_map/reduce_scatter | solution.py:64
  514.9 10.1 %copy-start = (f32[64,512]{1,0:T(8,128)}, f32[64,512]{1,0:T(8,128)S(1)}, u32[]{:S(2)}) copy-start(f32[64,512]{1,0:T(8,128)S(1)} %broadcast_multiply_fusion) | copy-start | bytes 393220
  514.9 5.1 collective-permute-start.2
  515.6 6.3 collective-permute-start.1
Sparse Core Ops, SparseCore 0:
  10.4 28.4 all-gather.3
  56.0 190.5 reduce-scatter.3
  249.9 75.4 all-gather.7
  327.7 23.3 all-gather.5
  361.3 152.6 reduce-scatter.5
  525.2 138.8 reduce-scatter.7
where the time goes:
time: 671 us
  waiting for transfers between devices  615 us (92%)
  matrix products  34.9 us (5%)
  between operations  14.2 us (2%)
    reduce_scatter x1, waiting for transfers between devices, on_device(): lax.psum_scatter(product(lower_rows.T, root_lower), 'grid', scatter_dimen...  189 us
    reduce_scatter x1, waiting for transfers between devices, on_device(): lax.psum_scatter(-product(cov_rows.T, factor), 'grid', scatter_dimension=...  153 us
    reduce_scatter x1, waiting for transfers between devices, on_device(): lax.psum_scatter(first - product(left_rows.T, factor), 'grid', scatter_di...  139 us
    all_gather x1, waiting for transfers between devices, on_device(): lax.all_gather(node_lower, 'grid', axis=0, tiled=True)  73.5 us
    dot_general x5, matrix products, product(): jnp.dot(left, right, precision=HIGHEST, preferred_element_type=jnp.float32)  34.9 us
    all_gather x1, waiting for transfers between devices, on_device(): lower_rows = lax.all_gather(root_lower, 'cube', axis=1, tiled=True)  29.8 us
    all_gather x1, waiting for transfers between devices, on_device(): cov_rows = lax.all_gather(root_cov, 'cube', axis=1, tiled=True)  22.7 us
  transfers between devices with their start and end apart: 9, of which 8 were waited for; matrix products, arithmetic and copies ran while one was open for 1% of the time, Pallas kernels for 0%

commit v1 on v0

v1 whole, which is shorter than its diff:
```python
import jax
import jax.numpy as jnp
from jax import lax
from jax.sharding import Mesh, PartitionSpec as P

BLK = 128
HIGHEST = lax.Precision.HIGHEST
XC = ("x", "c")


def shifted(value, axis, step):
    size = lax.axis_size(axis)
    return lax.ppermute(value, axis, [(i, (i + step) % size) for i in range(size)])


def from_partner(value, axis):
    return lax.ppermute(value, axis, [(i, i ^ 1) for i in range(lax.axis_size(axis))])


def gather(value, axis):
    size, me = lax.axis_size(axis), lax.axis_index(axis)
    out = jnp.zeros((size, *value.shape), value.dtype)
    rest = (0,) * value.ndim
    moved = [value] + [shifted(value, axis, step) for step in range(1, size)]
    for step, block in enumerate(moved):
        out = lax.dynamic_update_slice(out, block[None], ((me - step) % size, *rest))
    return out


def contract(spec, left, right):
    return jnp.einsum(spec, left, right, precision=HIGHEST, preferred_element_type=jnp.float32)


def lower_piece(weights, row_start, col_start):
    rows = row_start + lax.broadcasted_iota(jnp.int32, weights.shape, 0)
    cols = col_start + lax.broadcasted_iota(jnp.int32, weights.shape, 1)
    below = jnp.where(cols < rows, weights, jnp.zeros_like(weights))
    return below + jnp.where(cols == rows, 1.0, 0.0).astype(jnp.float32)


def join_halves(own, other, half, axis):
    first = jnp.concatenate([own, other], axis=axis)
    second = jnp.concatenate([other, own], axis=axis)
    return jnp.where(half == 0, first, second)


def on_device(root_inverse, level_inverse, coupling, pattern):
    y, z, x, c = (lax.axis_index(name) for name in ("y", "z", "x", "c"))
    ny, nz, nxc = lax.axis_size("y"), lax.axis_size("z"), lax.axis_size("x") * lax.axis_size("c")
    xc = x * lax.axis_size("c") + c
    grid_index = z * nxc + xc
    node, half = y // 2, y % 2
    rows, cols = root_inverse.shape
    node_rows, width = level_inverse.shape
    per_y = cols // (rows * nxc)

    root_lower = lower_piece(root_inverse, grid_index * rows, y * cols)
    node_lower = lower_piece(level_inverse, grid_index * node_rows, half * width)
    row_mask = pattern[node, grid_index * rows // BLK].astype(jnp.float32)

    coupled = gather(coupling * row_mask, "z").reshape(ny, per_y * rows, width)
    pieces = root_lower.reshape(rows, per_y, nxc, rows).transpose(2, 0, 1, 3).reshape(1, nxc, rows, per_y * rows)
    pieces = jnp.broadcast_to(pieces, (ny, *pieces.shape[1:])).reshape(ny * nxc, rows, per_y * rows)
    lower = lax.all_to_all(pieces, ("y", *XC), 0, 0, tiled=True).reshape(ny, nxc * rows, per_y * rows)
    lower_rows = lax.all_gather(root_lower, XC, axis=0, tiled=True)
    node_all = lax.all_gather(gather(node_lower, "z"), XC, axis=1, tiled=True)
    node_all = node_all.reshape(nz * nxc * node_rows, width)

    partial = contract("yrm,ymj->rj", lower, coupled).reshape(nxc, rows, width)
    mixed = jnp.sum(lax.all_to_all(partial, XC, 0, 0, tiled=True), axis=0)
    mixed = join_halves(mixed, from_partner(mixed, "y"), half, 1)
    solved = contract("rm,mj->rj", mixed, node_all)
    swapped = gather(solved, "x").reshape(-1, 1, rows, width)
    other = from_partner(swapped, "c")
    solved = join_halves(swapped, other, c, 1).reshape(nxc * rows, width)

    root = contract("yrm,rj->ymj", lower, lower_rows).reshape(nz * rows, cols)
    root_cov = lax.psum_scatter(root, "z", scatter_dimension=0, tiled=True)

    cross = contract("yrm,rj->ymj", lower, solved).reshape(nz, rows, width)
    own = lax.dynamic_index_in_dim(
        solved.reshape(nxc * rows, nz // 2, nxc, node_rows), xc, 2, keepdims=False
    ).reshape(nxc * rows, nz // 2 * node_rows)
    chosen = join_halves(own, from_partner(own, "y"), half, 1)
    gram = contract("rm,rj->mj", chosen, solved).reshape(nz, node_rows, width)
    both = jnp.concatenate([cross, gram], axis=1)
    both = lax.psum_scatter(both, "z", scatter_dimension=0, tiled=True)[0]
    cross_cov = -(both[:rows] * row_mask)
    mine = lax.dynamic_slice_in_dim(node_all, grid_index % (width // node_rows) * node_rows, node_rows, 1).T
    mine = jnp.where(grid_index // (width // node_rows) == half, mine, from_partner(mine, "y"))
    node_cov = contract("im,mj->ij", mine, node_all) + both[rows:]
    return root_cov, cross_cov, node_cov


def solution(mesh):
    split = Mesh(mesh.devices.reshape(4, 8, 4, 2), ("y", "z", "x", "c"))
    placed = P(("z", "x", "c"), "y")
    return jax.shard_map(
        on_device,
        mesh=split,
        in_specs=(placed, placed, placed, P()),
        out_specs=(placed, placed, placed),
        check_vma=False,
    )
```

time: 671 us -> 215 us (0.32)
  waiting for transfers between devices: 615 us -> 113 us
  starting transfers between devices: 2.93 us -> 52 us
  matrix products: 34.9 us -> 17.5 us
  local copies, waits for them, and re-layouts: 0.65 us -> 13.6 us
    reduce_scatter x3 -> x2, waiting for transfers between devices: 481 us -> 68.2 us  [the longest x1 39.5 us: on_device(): root_cov = lax.psum_scatter(root, 'z', scatter_dimension=0, tiled=True)]
    all_gather x3 -> x2, waiting for transfers between devices: 126 us -> 0.02 us  [the longest x1 0.02 us: on_device(): lower_rows = lax.all_gather(root_lower, XC, axis=0, tiled=True)]
    ppermute x3 -> x21, starting transfers between devices: 2.69 us -> 40.5 us  [the longest x17 34.9 us: shifted(): lax.ppermute(value, axis, [(i, (i + step) % size) for i in range(size)])]
    all_to_all x0 -> x2, waiting for transfers between devices: none -> 18.9 us  [the longest x1 15.2 us: on_device(): mixed = jnp.sum(lax.all_to_all(partial, XC, 0, 0, tiled=True), axis=0)]
    ppermute x3 -> x21, waiting for transfers between devices: 7.42 us -> 25 us  [the longest x17 17.8 us: shifted(): lax.ppermute(value, axis, [(i, (i + step) % size) for i in range(size)])]
    dot_general x5 -> x6, matrix products: 34.9 us -> 17.5 us  [contract(): jnp.einsum(spec, left, right, precision=HIGHEST, preferred_element_type=j...]
    all_to_all x0 -> x2, starting transfers between devices: none -> 11.3 us  [the longest x1 7.54 us: on_device(): lax.all_to_all(pieces, ('y', *XC), 0, 0, tiled=True)]
  transfers between devices with their start and end apart: 9 -> 27, of which waited for: 8 -> 14; matrix products, arithmetic and copies ran while one was open for 1% -> 15% of each run, Pallas kernels for 0% -> 0%
where the time goes in v1:
time: 215 us
  waiting for transfers between devices  113 us (53%)
  starting transfers between devices  52 us (24%)
  matrix products  17.5 us (8%)
  between operations  14.9 us (7%)
  local copies, waits for them, and re-layouts  13.6 us (6%)
  other arithmetic  3.97 us (2%)
    reduce_scatter x1, waiting for transfers between devices, on_device(): root_cov = lax.psum_scatter(root, 'z', scatter_dimension=0, tiled=True)  39.5 us
    ppermute x17, starting transfers between devices, shifted(): lax.ppermute(value, axis, [(i, (i + step) % size) for i in range(size)])  34.9 us
    reduce_scatter x1, waiting for transfers between devices, on_device(): both = lax.psum_scatter(both, 'z', scatter_dimension=0, tiled=True)[0]  28.7 us
    ppermute x17, waiting for transfers between devices, shifted(): lax.ppermute(value, axis, [(i, (i + step) % size) for i in range(size)])  17.8 us
    dot_general x6, matrix products, contract(): jnp.einsum(spec, left, right, precision=HIGHEST, preferred_element_type=j...  17.5 us
    all_to_all x1, waiting for transfers between devices, on_device(): mixed = jnp.sum(lax.all_to_all(partial, XC, 0, 0, tiled=True), axis=0)  15.2 us
    all_to_all x1, starting transfers between devices, on_device(): lax.all_to_all(pieces, ('y', *XC), 0, 0, tiled=True)  7.54 us
    ppermute x4, waiting for transfers between devices, from_partner(): lax.ppermute(value, axis, [(i, i ^ 1) for i in range(lax.axis_size(axis))])  7.16 us
  transfers between devices with their start and end apart: 27, of which 14 were waited for; matrix products, arithmetic and copies ran while one was open for 15% of the time, Pallas kernels for 0%

profile of v1, /device:TPU:8, one launch (start us, length us, event | category | flops | bytes accessed | tf_op | source)
XLA Modules:
  0.0 214.8 jit_solution(18180748498103813501)
XLA Ops:
  10.1 3.3 %collective-permute-start.9 = (f32[16,512]{1,0:T(8,128)S(1)}, f32[16,512]{1,0:T(8,128)S(1)}, u32[]{:S(2)}, u32[]{:S(2)}) collective-permute-start(f32[16,512]{1,0:T(8,128)S(1)} %get-tuple-element.6), channel_id=1, source_target_pairs={{0,16},{8,24},{16,32},{24,40},{32,48},{40,56},{48,0},{56,8},{1,17}... | collective-permute-start | bytes 98312 | tf_op jit(solution)/shard_map/ppermute | solution.py:13
  13.4 4.0 %collective-permute-start.10 = (f32[16,512]{1,0:T(8,128)S(1)}, f32[16,512]{1,0:T(8,128)S(1)}, u32[]{:S(2)}, u32[]{:S(2)}) collective-permute-start(f32[16,512]{1,0:T(8,128)S(1)} %get-tuple-element.6), channel_id=1, source_target_pairs={{0,24},{8,32},{16,40},{24,48},{32,56},{40,0},{48,8},{56,16},{1,25}... | collective-permute-start | bytes 98312 | tf_op jit(solution)/shard_map/ppermute | solution.py:13
  18.0 4.9 %collective-permute-start.12 = (f32[16,512]{1,0:T(8,128)S(1)}, f32[16,512]{1,0:T(8,128)S(1)}, u32[]{:S(2)}, u32[]{:S(2)}) collective-permute-start(f32[16,512]{1,0:T(8,128)S(1)} %get-tuple-element.6), channel_id=1, source_target_pairs={{0,40},{8,48},{16,56},{24,0},{32,8},{40,16},{48,24},{56,32},{1,41}... | collective-permute-start | bytes 98312 | tf_op jit(solution)/shard_map/ppermute | solution.py:13
  22.9 2.7 %collective-permute-start.13 = (f32[16,512]{1,0:T(8,128)S(1)}, f32[16,512]{1,0:T(8,128)S(1)}, u32[]{:S(2)}, u32[]{:S(2)}) collective-permute-start(f32[16,512]{1,0:T(8,128)S(1)} %get-tuple-element.6), channel_id=1, source_target_pairs={{0,48},{8,56},{16,0},{24,8},{32,16},{40,24},{48,32},{56,40},{1,49}... | collective-permute-start | bytes 98312 | tf_op jit(solution)/shard_map/ppermute | solution.py:13
  34.2 3.3 %collective-permute-start.2 = (f32[64,512]{1,0:T(8,128)S(1)}, f32[64,512]{1,0:T(8,128)S(1)}, u32[]{:S(2)}, u32[]{:S(2)}) collective-permute-start(f32[64,512]{1,0:T(8,128)S(1)} %get-tuple-element.4), channel_id=1, source_target_pairs={{0,24},{8,32},{16,40},{24,48},{32,56},{40,0},{48,8},{56,16},{1,25}... | collective-permute-start | bytes 393224 | tf_op jit(solution)/shard_map/ppermute | solution.py:13
  39.3 4.3 %collective-permute-start.4 = (f32[64,512]{1,0:T(8,128)S(1)}, f32[64,512]{1,0:T(8,128)S(1)}, u32[]{:S(2)}, u32[]{:S(2)}) collective-permute-start(f32[64,512]{1,0:T(8,128)S(1)} %get-tuple-element.4), channel_id=1, source_target_pairs={{0,40},{8,48},{16,56},{24,0},{32,8},{40,16},{48,24},{56,32},{1,41}... | collective-permute-start | bytes 393224 | tf_op jit(solution)/shard_map/ppermute | solution.py:13
  45.6 7.5 %all-to-all-start = ((f32[32,64,128]{2,1,0:T(8,128)}), f32[32,64,128]{2,1,0:T(8,128)S(1)}, u32[]{:S(2)}, u32[]{:S(2)}) async-start(f32[32,64,128]{2,1,0:T(8,128)} %bitcast.1), calls=%async_computation | async-start | bytes 2097152 | tf_op jit(solution)/shard_map/all_to_all | solution.py:64
  55.9 6.6 %collective-permute-done.5 = f32[64,512]{1,0:T(8,128)S(1)} collective-permute-done((f32[64,512]{1,0:T(8,128)S(1)}, f32[64,512]{1,0:T(8,128)S(1)}, u32[]{:S(2)}, u32[]{:S(2)}) %collective-permute-start.5) | collective-permute-done | bytes 131104 | tf_op jit(solution)/shard_map/ppermute | solution.py:13
  64.3 3.8 %all-to-all-done = f32[32,64,128]{2,1,0:T(8,128)S(1)} async-done(((f32[32,64,128]{2,1,0:T(8,128)}), f32[32,64,128]{2,1,0:T(8,128)S(1)}, u32[]{:S(2)}, u32[]{:S(2)}) %all-to-all-start) | async-done | bytes 1048608 | tf_op jit(solution)/shard_map/all_to_all | solution.py:64
  68.0 2.9 %convolution_bitcast_fusion = f32[8,64,512]{2,1,0:T(8,128)} fusion(f32[8,64,128,4]{2,1,0,3:T(8,128)S(1)} %bitcast.96, f32[4,128,512,1]{2,1,3,0:T(8,128)S(1)} %bitcast.98), kind=kOutput, calls=%fused_computation | convolution fusion | flops 1610612736 | bytes 3145728 | tf_op jit(solution)/shard_map/yrm,ymj->rj/dot_general | solution.py:31
  70.9 3.8 %all-to-all-start.1 = ((f32[8,64,512]{2,1,0:T(8,128)}), f32[8,64,512]{2,1,0:T(8,128)S(1)}, u32[]{:S(2)}, u32[]{:S(2)}) async-start(f32[8,64,512]{2,1,0:T(8,128)} %convolution_bitcast_fusion), calls=%async_computation.2 | async-start | bytes 2097152 | tf_op jit(solution)/shard_map/all_to_all | solution.py:70
  75.5 15.2 %all-to-all-done.1 = f32[8,64,512]{2,1,0:T(8,128)S(1)} async-done(((f32[8,64,512]{2,1,0:T(8,128)}), f32[8,64,512]{2,1,0:T(8,128)S(1)}, u32[]{:S(2)}, u32[]{:S(2)}) %all-to-all-start.1) | async-done | bytes 1048608 | tf_op jit(solution)/shard_map/all_to_all | solution.py:70
  90.8 2.4 %collective-permute-start.7 = (f32[64,512]{1,0:T(8,128)S(1)}, f32[64,512]{1,0:T(8,128)S(1)}, u32[]{:S(2)}, u32[]{:S(2)}) collective-permute-start(f32[64,512]{1,0:T(8,128)S(1)} %reduce_sum.9), channel_id=1, source_target_pairs={{0,64},{64,0},{128,192},{192,128},{1,65},{65,1},{129,193},{193,129... | collective-permute-start | bytes 393224 | tf_op jit(solution)/shard_map/ppermute | solution.py:17
  93.2 3.3 %collective-permute-done.7 = f32[64,512]{1,0:T(8,128)S(1)} collective-permute-done((f32[64,512]{1,0:T(8,128)S(1)}, f32[64,512]{1,0:T(8,128)S(1)}, u32[]{:S(2)}, u32[]{:S(2)}) %collective-permute-start.7) | collective-permute-done | bytes 131104 | tf_op jit(solution)/shard_map/ppermute | solution.py:17
  96.5 3.0 %bitcast_dynamic-update-slice_fusion.3 = (f32[4,1,64,512]{3,2,1,0:T(8,128)S(1)}, f32[64,512]{1,0:T(8,128)S(1)}) fusion(f32[4,1,64,512]{3,2,1,0:T(8,128)S(1)} %reshape.88, s32[]{:T(128)S(6)} %select_n.237, f32[1024,512]{1,0:T(8,128)} %bitcast.91, f32[64,512]{1,0:T(8,128)S(1)} %collective-permute-done.7, f32[64,512]{1,0:T(8,128)S(1)} %reduce_sum.9, pred[]{:T(512)S(6)} %eq.41), kind=kOutput, calls=%fused_computation.23 | convolution fusion | flops 402849792 | bytes 2621445 | tf_op jit(solution)/shard_map/rm,mj->rj/dot_general | solution.py:31
  100.2 2.1 collective-permute-start.16
  103.0 5.4 %collective-permute-done.15 = f32[64,512]{1,0:T(8,128)S(1)} collective-permute-done((f32[64,512]{1,0:T(8,128)S(1)}, f32[64,512]{1,0:T(8,128)S(1)}, u32[]{:S(2)}, u32[]{:S(2)}) %collective-permute-start.15) | collective-permute-done | bytes 131104 | tf_op jit(solution)/shard_map/ppermute | solution.py:13
  111.0 2.4 %copy.20 = f32[4,2,64,512]{2,1,0,3:T(2,128)} copy(f32[4,2,64,512]{3,2,1,0:T(8,128)S(1)} %maximum_select_fusion) | data formatting | bytes 2097152 | tf_op jit(solution)/shard_map/jit(_where)/select_n | solution.py:44
  113.4 4.1 %select_n.247 = f32[512,4,8,16]{0,3,2,1:T(8,128)} reshape(f32[4,2,64,512]{2,1,0,3:T(2,128)} %copy.20) | data formatting | bytes 2097152 | tf_op jit(solution)/shard_map/jit(_where)/select_n | solution.py:44
  121.9 2.3 %collective-permute-done.19 = f32[512,64]{0,1:T(8,128)S(1)} collective-permute-done((f32[512,64]{0,1:T(8,128)S(1)}, f32[512,64]{0,1:T(8,128)S(1)}, u32[]{:S(2)}, u32[]{:S(2)}) %collective-permute-start.19) | collective-permute-done | bytes 131104 | tf_op jit(solution)/shard_map/ppermute | solution.py:17
  126.3 6.5 %fusion.12 = f32[512,1024]{1,0:T(8,128)} fusion(f32[512,512]{1,0:T(8,128)S(1)} %bitcast.95, f32[512,1024]{1,0:T(8,128)} %all-gather.3.cloned.1.call-done), kind=kOutput, calls=%fused_computation.50 | convolution fusion | flops 3221225472 | bytes 5242880 | tf_op jit(solution)/shard_map/yrm,rj->ymj/dot_general | solution.py:31
  136.0 28.7 %reduce-scatter.5.cloned.1.call-done = f32[1,80,512]{2,1,0:T(8,128)} async-done(((f32[8,80,512]{2,1,0:T(8,128)}), f32[1,80,512]{2,1,0:T(8,128)}) %reduce-scatter.5.cloned.1.call-update) | async-done | bytes 163856 | tf_op jit(solution)/shard_map/reduce_scatter | solution.py:87
  166.3 2.5 %convolution_add_fusion = f32[16,512]{1,0:T(8,128)} fusion(f32[1024,512]{1,0:T(8,128)S(1)} %bitcast.93, f32[16,1024]{0,1:T(8,128)S(1)} %dynamic-slice_bitcast_fusion, f32[16,1024]{0,1:T(8,128)S(1)} %collective-permute-done.20, pred[]{:T(512)S(6)} %eq.43, f32[1,80,512]{2,1,0:T(8,128)} %reduce-scatter.5.cloned.1.call-done), kind=kOutput, calls=%fused_computation.2 | convolution fusion | flops 100687872 | bytes 2293761 | tf_op jit(solution)/shard_map/im,mj->ij/dot_general | solution.py:31
  168.8 39.5 %reduce-scatter.3.cloned.1.call-done = f32[64,1024]{1,0:T(8,128)} async-done(((f32[512,1024]{1,0:T(8,128)}), f32[64,1024]{1,0:T(8,128)}) %reduce-scatter.3.cloned.1.call-update) | async-done | bytes 262160 | tf_op jit(solution)/shard_map/reduce_scatter | solution.py:78
  (92 shorter events, 35.5 us)
Async XLA Ops:
  7.2 89.3 %all-gather.5.cloned.1.call-start = ((), (), s32[]{:S(2)}) async-start(), calls=%async_computation.6 | async-start | bytes 2359296 | tf_op jit(solution)/shard_map/all_gather | solution.py:66
  8.2 14.7 %collective-permute-start.8 = (f32[16,512]{1,0:T(8,128)S(1)}, f32[16,512]{1,0:T(8,128)S(1)}, u32[]{:S(2)}, u32[]{:S(2)}) collective-permute-start(f32[16,512]{1,0:T(8,128)S(1)} %get-tuple-element.6), channel_id=1, source_target_pairs={{0,8},{8,16},{16,24},{24,32},{32,40},{40,48},{48,56},{56,0},{1,9},... | collective-permute-start | bytes 98312 | tf_op jit(solution)/shard_map/ppermute | solution.py:13
  10.1 15.5 %collective-permute-start.9 = (f32[16,512]{1,0:T(8,128)S(1)}, f32[16,512]{1,0:T(8,128)S(1)}, u32[]{:S(2)}, u32[]{:S(2)}) collective-permute-start(f32[16,512]{1,0:T(8,128)S(1)} %get-tuple-element.6), channel_id=1, source_target_pairs={{0,16},{8,24},{16,32},{24,40},{32,48},{40,56},{48,0},{56,8},{1,17}... | collective-permute-start | bytes 98312 | tf_op jit(solution)/shard_map/ppermute | solution.py:13
  13.4 13.3 %collective-permute-start.10 = (f32[16,512]{1,0:T(8,128)S(1)}, f32[16,512]{1,0:T(8,128)S(1)}, u32[]{:S(2)}, u32[]{:S(2)}) collective-permute-start(f32[16,512]{1,0:T(8,128)S(1)} %get-tuple-element.6), channel_id=1, source_target_pairs={{0,24},{8,32},{16,40},{24,48},{32,56},{40,0},{48,8},{56,16},{1,25}... | collective-permute-start | bytes 98312 | tf_op jit(solution)/shard_map/ppermute | solution.py:13
  17.4 9.3 %collective-permute-start.11 = (f32[16,512]{1,0:T(8,128)S(1)}, f32[16,512]{1,0:T(8,128)S(1)}, u32[]{:S(2)}, u32[]{:S(2)}) collective-permute-start(f32[16,512]{1,0:T(8,128)S(1)} %get-tuple-element.6), channel_id=1, source_target_pairs={{0,32},{8,40},{16,48},{24,56},{32,0},{40,8},{48,16},{56,24},{1,33}... | collective-permute-start | bytes 98312 | tf_op jit(solution)/shard_map/ppermute | solution.py:13
  18.0 8.8 %collective-permute-start.12 = (f32[16,512]{1,0:T(8,128)S(1)}, f32[16,512]{1,0:T(8,128)S(1)}, u32[]{:S(2)}, u32[]{:S(2)}) collective-permute-start(f32[16,512]{1,0:T(8,128)S(1)} %get-tuple-element.6), channel_id=1, source_target_pairs={{0,40},{8,48},{16,56},{24,0},{32,8},{40,16},{48,24},{56,32},{1,41}... | collective-permute-start | bytes 98312 | tf_op jit(solution)/shard_map/ppermute | solution.py:13
  32.4 20.7 %collective-permute-start = (f32[64,512]{1,0:T(8,128)S(1)}, f32[64,512]{1,0:T(8,128)S(1)}, u32[]{:S(2)}, u32[]{:S(2)}) collective-permute-start(f32[64,512]{1,0:T(8,128)S(1)} %get-tuple-element.4), channel_id=1, source_target_pairs={{0,8},{8,16},{16,24},{24,32},{32,40},{40,48},{48,56},{56,0},{1,9},... | collective-permute-start | bytes 393224 | tf_op jit(solution)/shard_map/ppermute | solution.py:13
  32.5 21.8 %collective-permute-start.1 = (f32[64,512]{1,0:T(8,128)S(1)}, f32[64,512]{1,0:T(8,128)S(1)}, u32[]{:S(2)}, u32[]{:S(2)}) collective-permute-start(f32[64,512]{1,0:T(8,128)S(1)} %get-tuple-element.4), channel_id=1, source_target_pairs={{0,16},{8,24},{16,32},{24,40},{32,48},{40,56},{48,0},{56,8},{1,17}... | collective-permute-start | bytes 393224 | tf_op jit(solution)/shard_map/ppermute | solution.py:13
  34.2 20.8 %collective-permute-start.2 = (f32[64,512]{1,0:T(8,128)S(1)}, f32[64,512]{1,0:T(8,128)S(1)}, u32[]{:S(2)}, u32[]{:S(2)}) collective-permute-start(f32[64,512]{1,0:T(8,128)S(1)} %get-tuple-element.4), channel_id=1, source_target_pairs={{0,24},{8,32},{16,40},{24,48},{32,56},{40,0},{48,8},{56,16},{1,25}... | collective-permute-start | bytes 393224 | tf_op jit(solution)/shard_map/ppermute | solution.py:13
  37.5 18.4 %collective-permute-start.3 = (f32[64,512]{1,0:T(8,128)S(1)}, f32[64,512]{1,0:T(8,128)S(1)}, u32[]{:S(2)}, u32[]{:S(2)}) collective-permute-start(f32[64,512]{1,0:T(8,128)S(1)} %get-tuple-element.4), channel_id=1, source_target_pairs={{0,32},{8,40},{16,48},{24,56},{32,0},{40,8},{48,16},{56,24},{1,33}... | collective-permute-start | bytes 393224 | tf_op jit(solution)/shard_map/ppermute | solution.py:13
  39.3 16.6 %collective-permute-start.4 = (f32[64,512]{1,0:T(8,128)S(1)}, f32[64,512]{1,0:T(8,128)S(1)}, u32[]{:S(2)}, u32[]{:S(2)}) collective-permute-start(f32[64,512]{1,0:T(8,128)S(1)} %get-tuple-element.4), channel_id=1, source_target_pairs={{0,40},{8,48},{16,56},{24,0},{32,8},{40,16},{48,24},{56,32},{1,41}... | collective-permute-start | bytes 393224 | tf_op jit(solution)/shard_map/ppermute | solution.py:13
  45.6 22.5 %all-to-all-start = ((f32[32,64,128]{2,1,0:T(8,128)}), f32[32,64,128]{2,1,0:T(8,128)S(1)}, u32[]{:S(2)}, u32[]{:S(2)}) async-start(f32[32,64,128]{2,1,0:T(8,128)} %bitcast.1), calls=%async_computation | async-start | bytes 2097152 | tf_op jit(solution)/shard_map/all_to_all | solution.py:64
  53.1 9.4 %collective-permute-start.5 = (f32[64,512]{1,0:T(8,128)S(1)}, f32[64,512]{1,0:T(8,128)S(1)}, u32[]{:S(2)}, u32[]{:S(2)}) collective-permute-start(f32[64,512]{1,0:T(8,128)S(1)} %get-tuple-element.4), channel_id=1, source_target_pairs={{0,48},{8,56},{16,0},{24,8},{32,16},{40,24},{48,32},{56,40},{1,49}... | collective-permute-start | bytes 393224 | tf_op jit(solution)/shard_map/ppermute | solution.py:13
  54.3 9.9 %collective-permute-start.6 = (f32[64,512]{1,0:T(8,128)S(1)}, f32[64,512]{1,0:T(8,128)S(1)}, u32[]{:S(2)}, u32[]{:S(2)}) collective-permute-start(f32[64,512]{1,0:T(8,128)S(1)} %get-tuple-element.4), channel_id=1, source_target_pairs={{0,56},{8,0},{16,8},{24,16},{32,24},{40,32},{48,40},{56,48},{1,57}... | collective-permute-start | bytes 393224 | tf_op jit(solution)/shard_map/ppermute | solution.py:13
  70.9 19.8 %all-to-all-start.1 = ((f32[8,64,512]{2,1,0:T(8,128)}), f32[8,64,512]{2,1,0:T(8,128)S(1)}, u32[]{:S(2)}, u32[]{:S(2)}) async-start(f32[8,64,512]{2,1,0:T(8,128)} %convolution_bitcast_fusion), calls=%async_computation.2 | async-start | bytes 2097152 | tf_op jit(solution)/shard_map/all_to_all | solution.py:70
  74.7 51.5 %all-gather.3.cloned.1.call-start = ((), (), s32[]{:S(2)}) async-start(), calls=%async_computation.4 | async-start | bytes 2359296 | tf_op jit(solution)/shard_map/all_gather | solution.py:65
  75.5 89.3 %reduce-scatter.5.cloned.1.call-start = ((), (), s32[]{:S(2)}) async-start(), calls=%async_computation.7 | async-start | bytes 1474560 | tf_op jit(solution)/shard_map/reduce_scatter | solution.py:87
  90.8 5.7 %collective-permute-start.7 = (f32[64,512]{1,0:T(8,128)S(1)}, f32[64,512]{1,0:T(8,128)S(1)}, u32[]{:S(2)}, u32[]{:S(2)}) collective-permute-start(f32[64,512]{1,0:T(8,128)S(1)} %reduce_sum.9), channel_id=1, source_target_pairs={{0,64},{64,0},{128,192},{192,128},{1,65},{65,1},{129,193},{193,129... | collective-permute-start | bytes 393224 | tf_op jit(solution)/shard_map/ppermute | solution.py:17
  99.5 8.9 %collective-permute-start.15 = (f32[64,512]{1,0:T(8,128)S(1)}, f32[64,512]{1,0:T(8,128)S(1)}, u32[]{:S(2)}, u32[]{:S(2)}) collective-permute-start(f32[64,512]{1,0:T(8,128)S(1)} %get-tuple-element.8), channel_id=1, source_target_pairs={{0,2},{2,4},{4,6},{6,0},{1,3},{3,5},{5,7},{7,1},{8,10},{10,12},{12... | collective-permute-start | bytes 393224 | tf_op jit(solution)/shard_map/ppermute | solution.py:13
  100.2 8.3 %collective-permute-start.16 = (f32[64,512]{1,0:T(8,128)S(1)}, f32[64,512]{1,0:T(8,128)S(1)}, u32[]{:S(2)}, u32[]{:S(2)}) collective-permute-start(f32[64,512]{1,0:T(8,128)S(1)} %get-tuple-element.8), channel_id=1, source_target_pairs={{0,4},{2,6},{4,0},{6,2},{1,5},{3,7},{5,1},{7,3},{8,12},{10,14},{12... | collective-permute-start | bytes 393224 | tf_op jit(solution)/shard_map/ppermute | solution.py:13
  102.2 6.6 %collective-permute-start.17 = (f32[64,512]{1,0:T(8,128)S(1)}, f32[64,512]{1,0:T(8,128)S(1)}, u32[]{:S(2)}, u32[]{:S(2)}) collective-permute-start(f32[64,512]{1,0:T(8,128)S(1)} %get-tuple-element.8), channel_id=1, source_target_pairs={{0,6},{2,0},{4,2},{6,4},{1,7},{3,1},{5,3},{7,5},{8,14},{10,8},{12,... | collective-permute-start | bytes 393224 | tf_op jit(solution)/shard_map/ppermute | solution.py:13
  118.4 5.8 %collective-permute-start.19 = (f32[512,64]{0,1:T(8,128)S(1)}, f32[512,64]{0,1:T(8,128)S(1)}, u32[]{:S(2)}, u32[]{:S(2)}) collective-permute-start(f32[512,64]{0,1:T(8,128)S(1)} %bitcast.101), channel_id=1, source_target_pairs={{0,64},{64,0},{128,192},{192,128},{1,65},{65,1},{129,193},{193,129... | collective-permute-start | bytes 393224 | tf_op jit(solution)/shard_map/ppermute | solution.py:17
  126.2 82.1 %reduce-scatter.3.cloned.1.call-start = ((), (), s32[]{:S(2)}) async-start(), calls=%async_computation.5 | async-start | bytes 2359296 | tf_op jit(solution)/shard_map/reduce_scatter | solution.py:78
  134.6 31.7 %collective-permute-start.20 = (f32[16,1024]{0,1:T(8,128)S(1)}, f32[16,1024]{0,1:T(8,128)S(1)}, u32[]{:S(2)}, u32[]{:S(2)}) collective-permute-start(f32[16,1024]{0,1:T(8,128)S(1)} %dynamic-slice_bitcast_fusion), channel_id=1, source_target_pairs={{0,64},{64,0},{128,192},{192,128},{1,65},{65,1},{129,193},{193,129... | collective-permute-start | bytes 196616 | tf_op jit(solution)/shard_map/ppermute | solution.py:17
  (8 other events, 76.8 us)
Sparse Core Ops, SparseCore 0:
  30.4 25.5 all-gather.4
  78.0 26.6 all-gather.2
  126.3 38.3 reduce-scatter.4
  167.7 40.5 reduce-scatter.2

commit v2 on v1

v2 whole, which is shorter than its diff:
```python
import jax
import jax.numpy as jnp
from jax import lax
from jax.experimental import pallas as pl
from jax.experimental.pallas import tpu as pltpu
from jax.sharding import Mesh, PartitionSpec as P

BLK = 128
NY, NZ, NX, NC = 4, 8, 4, 2
NXC = NX * NC
F32 = jnp.float32


def shifted(value, axis, step):
    size = lax.axis_size(axis)
    return lax.ppermute(value, axis, [(i, (i + step) % size) for i in range(size)])


def from_partner(value, axis):
    return lax.ppermute(value, axis, [(i, i ^ 1) for i in range(lax.axis_size(axis))])


def chip_blocks(value):
    own = [value] + [shifted(value, "x", s) for s in range(1, NX)]
    return own + [from_partner(block, "c") for block in own]


def halves(value):
    high = value.astype(jnp.bfloat16)
    return high, (value - high.astype(F32)).astype(jnp.bfloat16)


def product(left, right, contracting):
    (high, low), (right_high, right_low) = halves(left), halves(right)

    def dot(p, q):
        return lax.dot_general(p, q, (contracting, ((), ())), preferred_element_type=F32)

    return dot(high, right_high) + (dot(high, right_low) + dot(low, right_high))


ROWS = ((1,), (0,))
COLS = ((0,), (0,))


def call(body, outs, scratch=(), n_in=1, aliases=None, in_specs=None, out_specs=None, grid=(), copies=0):
    vmem = pl.BlockSpec(memory_space=pltpu.VMEM)
    smem = pl.BlockSpec(memory_space=pltpu.SMEM)
    return pl.pallas_call(
        body,
        out_shape=[jax.ShapeDtypeStruct(shape, F32) for shape in outs],
        in_specs=in_specs or [smem] + [vmem] * n_in,
        out_specs=out_specs or [vmem] * len(outs),
        grid=grid,
        scratch_shapes=[pltpu.VMEM(shape, F32) for shape in scratch]
        + ([pltpu.SemaphoreType.DMA((copies,))] if copies else []),
        input_output_aliases=aliases or {},
        compiler_params=pltpu.CompilerParams(vmem_limit_bytes=48 * 2**20),
    )


def lower_piece(weights, row_start, col_start):
    rows = row_start + lax.broadcasted_iota(jnp.int32, weights.shape, 0)
    cols = col_start + lax.broadcasted_iota(jnp.int32, weights.shape, 1)
    below = jnp.where(cols < rows, weights, 0.0)
    return below + jnp.where(cols == rows, 1.0, 0.0).astype(F32)


def row_mask(at, pattern, rows):
    block = (at[1] * NXC + at[2] * NC + at[3]) * rows // BLK
    return pattern[at[0] // 2, block].astype(F32)


def stack_rows(at, pattern, level, coupling, after, stacks, nodes, rows_in, sem):
    del after
    moves = [pltpu.make_async_copy(level, nodes, sem.at[0]), pltpu.make_async_copy(coupling, rows_in, sem.at[1])]
    for move in moves:
        move.start()
    for move in moves:
        move.wait()
    rows, g = coupling.shape[0], at[1] * NXC + at[2] * NC + at[3]
    masked = rows_in[...] * row_mask(at, pattern, rows)
    low = lower_piece(nodes[...], g * level.shape[0], at[0] % 2 * level.shape[1])
    for to in range(NZ):
        stacks[to, :rows] = masked
        stacks[to, rows:] = low


def root_columns(at, *refs):
    blocks, (whole, columns) = refs[:NXC], refs[NXC:]
    rows, cols = blocks[0].shape
    for k, block in enumerate(blocks):
        core = at[3] if k < NX else 1 - at[3]
        place = lax.rem(at[2] + NX - k % NX, NX) * NC + core
        low = lower_piece(block[...], (at[1] * NXC + place) * rows, at[0] * cols)
        whole[pl.ds(pl.multiple_of(place * rows, rows), rows)] = low
    parts = []
    for b in range(0, cols, NXC * rows):
        pair = whole[:, pl.ds(pl.multiple_of(b + at[2] * NC * rows, NC * rows), NC * rows)]
        parts.append(jnp.where(at[3] == 0, pair[:, :rows], pair[:, rows:]))
    columns[...] = jnp.concatenate(parts, axis=1)


def whole_lower(columns):
    return jnp.concatenate([block[...] for block in columns], axis=1)


def place_chip_blocks(at, blocks, out):
    rows = blocks[0].shape[0]
    for k, block in enumerate(blocks):
        s, core = k % NX, at[3] if k < NX else 1 - at[3]
        chip = lax.rem(at[2] + NX - s, NX)
        out[pl.ds(pl.multiple_of((chip * NC + core) * rows, rows), rows)] = block[...]


def mix(at, *refs):
    columns, stacks, (keep, give, nodes, full, part) = refs[:NY], refs[NY], refs[NY + 2:]
    rows, per_y = keep.shape[1], NZ // NY
    for s in range(NY):
        k = lax.rem(at[0] + NY - s, NY) * per_y
        for b in range(per_y):
            full[(s * per_y + b) * rows:(s * per_y + b + 1) * rows] = stacks[k + b, :rows]
    nodes[...] = stacks[:, rows:]
    part[...] = product(whole_lower(columns), full[...], ROWS)
    for s in range(NX):
        chip = lax.rem(at[2] + NX - s, NX)
        for core, out in ((at[3], keep), (1 - at[3], give)):
            out[s] = part[pl.ds(pl.multiple_of((chip * NC + core) * rows, rows), rows)]


def add_cores(at, keep, got, *outs):
    for s, out in enumerate(outs):
        out[...] = keep[s] + got[s]


def whole_node(at, *refs):
    blocks, out = refs[:NXC], refs[NXC]
    for k, block in enumerate(blocks):
        s, core = k % NX, at[3] if k < NX else 1 - at[3]
        chip = lax.rem(at[2] + NX - s, NX)
        for b in range(NZ):
            out[b, chip * NC + core] = block[b]


def solve(at, own, other, node, out):
    half = at[0] % 2
    width = own.shape[1]
    first = node[pl.ds(pl.multiple_of(half * width, width), width)]
    second = node[pl.ds(pl.multiple_of((1 - half) * width, width), width)]
    out[...] = product(own[...], first, ROWS) + product(other[...], second, ROWS)


def store_by_y(at, value, out, rows):
    per_y = NZ // NY
    for s in range(NY):
        k = lax.rem(at[0] + NY - s, NY) * per_y
        for b in range(per_y):
            at_row = (s * per_y + b) * rows
            out[k + b, :rows] = value[at_row:at_row + rows]


def root_product(at, *refs):
    columns, (whole, out) = refs[:NY], refs[NY:]
    store_by_y(at, product(whole_lower(columns), whole[...], COLS), out, out.shape[1])


def choose(at, *refs):
    blocks, (out, full) = refs[:NXC], refs[NXC:]
    place_chip_blocks(at, blocks, full)
    size, take = out.shape[0], out.shape[1] // 2
    node_rows = take * 2 // NZ
    src = lax.broadcasted_iota(jnp.int32, (full.shape[1], take), 0)
    dst = lax.broadcasted_iota(jnp.int32, (full.shape[1], take), 1)
    pick = src == dst // node_rows * (NXC * node_rows) + (at[2] * NC + at[3]) * node_rows + dst % node_rows
    taken = product(full[...], jnp.where(pick, 1.0, 0.0).astype(F32), ROWS)
    out[...] = jnp.concatenate([taken[:size], taken[size:]], axis=1)


def cross_product(at, *refs):
    columns, blocks, (out, full) = refs[:NY], refs[NY:NY + NXC], refs[NY + NXC:]
    place_chip_blocks(at, blocks, full)
    store_by_y(at, product(whole_lower(columns), full[...], COLS), out, blocks[0].shape[0])


def gram_product(at, own, other, *refs):
    blocks, (_, out, full) = refs[:NXC], refs[NXC:]
    place_chip_blocks(at, blocks, full)
    first, take = (at[0] % 2) == 0, own.shape[1] // 2
    mine, his = own[...], other[...]
    low, high = jnp.where(first, mine, his), jnp.where(first, his, mine)
    chosen = jnp.concatenate(
        [
            jnp.concatenate([low[:, :take], high[:, :take]], axis=1),
            jnp.concatenate([low[:, take:], high[:, take:]], axis=1),
        ],
        axis=0,
    )
    out[...] = product(chosen, full[...], COLS).reshape(out.shape)


def finish(at, pattern, got, gram, cross, node):
    total = got[0]
    for k in range(1, NZ):
        total = total + got[k]
    rows = cross.shape[0]
    cross[...] = -(total[:rows] * row_mask(at, pattern, rows))
    node[...] = gram[...] + total[rows:]


def on_device(root_inverse, level_inverse, coupling, pattern):
    y, z, x, c = (lax.axis_index(name) for name in ("y", "z", "x", "c"))
    grid_index = z * NXC + x * NC + c
    half = y % 2
    rows, cols = root_inverse.shape
    node_rows, width = level_inverse.shape
    at = jnp.stack([y, z, x, c]).astype(jnp.int32)
    per = rows + node_rows
    smem, vmem, anywhere = (pl.BlockSpec(memory_space=m) for m in (pltpu.SMEM, pltpu.VMEM, pl.ANY))

    blocks = chip_blocks(root_inverse)
    stacks = call(
        stack_rows,
        [(NZ, per, width)],
        [(node_rows, width), (rows, width)],
        in_specs=[smem, smem, anywhere, anywhere, anywhere],
        copies=2,
    )(at, pattern, level_inverse, coupling, level_inverse)[0]
    stacks = lax.all_to_all(stacks, "z", 0, 0, tiled=True)
    whole, columns = call(root_columns, [(NXC * rows, cols), (NXC * rows, cols // NXC)], n_in=NXC)(
        at, *blocks
    )
    columns = [columns] + [shifted(columns, "y", s) for s in range(1, NY)]

    root = call(root_product, [(NZ, rows, cols)], n_in=NY + 1)(
        at, *columns, whole
    )[0]
    summed = lax.all_to_all(root, "z", 0, 0, tiled=True)

    keep, give, nodes = call(
        mix,
        [(NX, rows, width), (NX, rows, width), (NZ, node_rows, width)],
        [(NZ * rows, width), (NXC * rows, width)],
        in_specs=[smem] + [vmem] * (NY + 1) + [anywhere],
    )(at, *columns, stacks, root)
    parts = call(add_cores, [(rows, width)] * NX, n_in=2)(at, keep, from_partner(give, "c"))
    mixed = parts[0]
    for s in range(1, NX):
        mixed = mixed + shifted(parts[s], "x", -s)

    node_all = call(whole_node, [(NZ, NXC, node_rows, width)], n_in=NXC)(at, *chip_blocks(nodes))[0]
    node_all = node_all.reshape(NZ * NXC * node_rows, width)
    solved = call(solve, [(rows, width)], n_in=3)(at, mixed, from_partner(mixed, "y"), node_all)[0]
    solved = chip_blocks(solved)

    own = call(choose, [(NX * rows, 2 * width // NXC)], [(NXC * rows, width)], NXC)(at, *solved)[0]
    both = call(cross_product, [(NZ, per, width)], [(NXC * rows, width)], NY + NXC)(at, *columns, *solved)[0]
    both = call(
        gram_product,
        [(NZ, per, width)],
        [(NXC * rows, width)],
        aliases={3 + NXC: 0},
        in_specs=[smem] + [vmem] * (2 + NXC) + [anywhere],
        out_specs=[pl.BlockSpec((NZ, node_rows, width), lambda i: (0, rows // node_rows, 0))],
        grid=(1,),
    )(at, own, from_partner(own, "y"), *solved, both)[0]
    both, summed = lax.optimization_barrier((both, summed))
    both = lax.all_to_all(both, "z", 0, 0, tiled=True)

    per_half = width // node_rows
    mine = lax.dynamic_slice_in_dim(node_all, grid_index % per_half * node_rows, node_rows, 1).T
    mine = jnp.where(grid_index // per_half == half, mine, from_partner(mine, "y"))
    node_gram = jnp.dot(mine, node_all, precision=lax.Precision.HIGHEST, preferred_element_type=F32)
    cross_cov, node_cov = call(finish, [(rows, width), (node_rows, width)], in_specs=[smem, smem, vmem, vmem])(
        at, pattern, both, node_gram
    )
    return jnp.sum(summed, axis=0), cross_cov, node_cov


def solution(mesh):
    split = Mesh(mesh.devices.reshape(NY, NZ, NX, NC), ("y", "z", "x", "c"))
    placed = P(("z", "x", "c"), "y")
    return jax.shard_map(
        on_device,
        mesh=split,
        in_specs=(placed, placed, placed, P()),
        out_specs=(placed, placed, placed),
        check_vma=False,
    )
```

time: 215 us -> 154 us (0.72)
  waiting for transfers between devices: 113 us -> 77.2 us
  Pallas kernels: 0 us -> 18.1 us
  matrix products: 17.5 us -> 2.18 us
  between operations: 14.9 us -> 0.76 us
  local copies, waits for them, and re-layouts: 13.6 us -> 3.36 us
  starting transfers between devices: 52 us -> 48.1 us
    reduce_scatter x2 -> x0, waiting for transfers between devices: 68.2 us -> none  [the longest x1 39.5 us: on_device(): root_cov = lax.psum_scatter(root, 'z', scatter_dimension=0, tiled=True)]
    ppermute x17 -> x15, waiting for transfers between devices: 17.8 us -> 40.7 us  [shifted(): lax.ppermute(value, axis, [(i, (i + step) % size) for i in range(size)])]
    pallas_call x0 -> x11, Pallas kernels: none -> 18.1 us  [the longest x1 3.75 us: on_device(): call(root_product, [(NZ, rows, cols)], n_in=NY + 1)(at, *columns, whole)[0]]
    dot_general x6 -> x1, matrix products: 17.5 us -> 2.18 us  [on_device(): jnp.dot(mine, node_all, precision=lax.Precision.HIGHEST, preferred_elemen...]
    ppermute x4 -> x16, waiting for transfers between devices: 7.16 us -> 21.2 us  [from_partner(): lax.ppermute(value, axis, [(i, i ^ 1) for i in range(lax.axis_size(axis))])]
    ppermute x17 -> x15, starting transfers between devices: 34.9 us -> 22 us  [shifted(): lax.ppermute(value, axis, [(i, (i + step) % size) for i in range(size)])]
    all_to_all x2 -> x3, starting transfers between devices: 11.3 us -> 22.2 us  [the longest x1 8.48 us: on_device(): stacks = lax.all_to_all(stacks, 'z', 0, 0, tiled=True)]
    select_n x2 -> x0, local copies, waits for them, and re-layouts: 6.45 us -> none  [join_halves(): return jnp.where(half == 0, first, second)]
  transfers between devices with their start and end apart: 27 -> 34, of which waited for: 14 -> 24; matrix products, arithmetic and copies ran while one was open for 15% -> 4% of each run, Pallas kernels for 0% -> 10%
where the time goes in v2:
time: 154 us; the launch traced here: 152 us
  waiting for transfers between devices  77.2 us (50%)
  starting transfers between devices  48.1 us (31%)
  Pallas kernels  18.1 us (12%)
  local copies, waits for them, and re-layouts  3.36 us (2%)
  other arithmetic  2.57 us (2%)
  matrix products  2.18 us (1%)
    ppermute x15, waiting for transfers between devices, shifted(): lax.ppermute(value, axis, [(i, (i + step) % size) for i in range(size)])  40.7 us
    ppermute x15, starting transfers between devices, shifted(): lax.ppermute(value, axis, [(i, (i + step) % size) for i in range(size)])  22 us
    ppermute x16, waiting for transfers between devices, from_partner(): lax.ppermute(value, axis, [(i, i ^ 1) for i in range(lax.axis_size(axis))])  21.2 us
    all_to_all x1, waiting for transfers between devices, on_device(): both = lax.all_to_all(both, 'z', 0, 0, tiled=True)  15 us
    all_to_all x1, starting transfers between devices, on_device(): stacks = lax.all_to_all(stacks, 'z', 0, 0, tiled=True)  8.48 us
    all_to_all x1, starting transfers between devices, on_device(): both = lax.all_to_all(both, 'z', 0, 0, tiled=True)  6.89 us
    all_to_all x1, starting transfers between devices, on_device(): summed = lax.all_to_all(root, 'z', 0, 0, tiled=True)  6.85 us
    ppermute x16, starting transfers between devices, from_partner(): lax.ppermute(value, axis, [(i, i ^ 1) for i in range(lax.axis_size(axis))])  3.87 us
  transfers between devices with their start and end apart: 34, of which 24 were waited for; matrix products, arithmetic and copies ran while one was open for 4% of the time, Pallas kernels for 10%

profile of v2, /device:TPU:8, one launch (start us, length us, event | category | flops | bytes accessed | tf_op | source)
XLA Modules:
  0.0 152.2 jit_solution(3233505272246868998)
XLA Ops:
  5.1 8.5 %all-to-all-start = ((f32[8,80,512]{2,1,0:T(8,128)}), f32[8,80,512]{2,1,0:T(8,128)S(1)}, u32[]{:S(2)}, u32[]{:S(2)}) async-start(f32[8,80,512]{2,1,0:T(8,128)} %shard_map.68), calls=%async_computation | async-start | bytes 2621440 | tf_op jit(solution)/shard_map/all_to_all | solution.py:228
  15.1 2.7 %collective-permute-start.1 = (f32[64,1024]{1,0:T(8,128)S(1)}, f32[64,1024]{1,0:T(8,128)S(1)}, u32[]{:S(2)}, u32[]{:S(2)}) collective-permute-start(f32[64,1024]{1,0:T(8,128)S(1)} %copy-done), channel_id=1, source_target_pairs={{0,4},{2,6},{4,0},{6,2},{1,5},{3,7},{5,1},{7,3},{8,12},{10,14},{12... | collective-permute-start | bytes 786440 | tf_op jit(solution)/shard_map/ppermute | solution.py:16
  19.3 3.8 %collective-permute-done.refs_1_ = f32[64,1024]{1,0:T(8,128)S(1)} collective-permute-done((f32[64,1024]{1,0:T(8,128)S(1)}, f32[64,1024]{1,0:T(8,128)S(1)}, u32[]{:S(2)}, u32[]{:S(2)}) %collective-permute-start) | collective-permute-done | bytes 262176 | tf_op jit(solution)/shard_map/ppermute | solution.py:16
  23.1 6.1 %collective-permute-done.1.refs_2_ = f32[64,1024]{1,0:T(8,128)S(1)} collective-permute-done((f32[64,1024]{1,0:T(8,128)S(1)}, f32[64,1024]{1,0:T(8,128)S(1)}, u32[]{:S(2)}, u32[]{:S(2)}) %collective-permute-start.1) | collective-permute-done | bytes 262176 | tf_op jit(solution)/shard_map/ppermute | solution.py:16
  35.0 2.4 %collective-permute-start.9 = (f32[512,128]{1,0:T(8,128)S(1)}, f32[512,128]{1,0:T(8,128)S(1)}, u32[]{:S(2)}, u32[]{:S(2)}) collective-permute-start(f32[512,128]{1,0:T(8,128)S(1)} %get-tuple-element.16.refs_0_), channel_id=1, source_target_pairs={{0,192},{64,0},{128,64},{192,128},{1,193},{65,1},{129,65},{193,129... | collective-permute-start | bytes 786440 | tf_op jit(solution)/shard_map/ppermute | solution.py:16
  37.4 4.2 %collective-permute-done.7.refs_1_ = f32[512,128]{1,0:T(8,128)S(1)} collective-permute-done((f32[512,128]{1,0:T(8,128)S(1)}, f32[512,128]{1,0:T(8,128)S(1)}, u32[]{:S(2)}, u32[]{:S(2)}) %collective-permute-start.7) | collective-permute-done | bytes 262176 | tf_op jit(solution)/shard_map/ppermute | solution.py:16
  41.6 3.1 %collective-permute-done.8.refs_2_ = f32[512,128]{1,0:T(8,128)S(1)} collective-permute-done((f32[512,128]{1,0:T(8,128)S(1)}, f32[512,128]{1,0:T(8,128)S(1)}, u32[]{:S(2)}, u32[]{:S(2)}) %collective-permute-start.8) | collective-permute-done | bytes 262176 | tf_op jit(solution)/shard_map/ppermute | solution.py:16
  44.7 3.8 %collective-permute-done.9.refs_3_ = f32[512,128]{1,0:T(8,128)S(1)} collective-permute-done((f32[512,128]{1,0:T(8,128)S(1)}, f32[512,128]{1,0:T(8,128)S(1)}, u32[]{:S(2)}, u32[]{:S(2)}) %collective-permute-start.9) | collective-permute-done | bytes 262176 | tf_op jit(solution)/shard_map/ppermute | solution.py:16
  48.5 3.8 %shard_map.69.refs_5_ = f32[8,64,1024]{2,1,0:T(8,128)} custom-call(s32[4]{0:T(128)S(1)} %pad_add_fusion.at, f32[512,128]{1,0:T(8,128)S(1)} %get-tuple-element.16.refs_0_, f32[512,128]{1,0:T(8,128)S(1)} %collective-permute-done.7.refs_1_, f32[512,128]{1,0:T(8,128)S(1)} %collective-permute-done.8.refs_2_, f32[512,128]{1,0:T(8,128)S(1)} %collective-permute-done.9.refs_3_, ...), custom_call_target="tpu_custom_call" | custom-call | tf_op jit(solution)/shard_map/pallas_call | solution.py:234
  52.3 6.9 %all-to-all-start.1 = ((f32[8,64,1024]{2,1,0:T(8,128)}), f32[8,64,1024]{2,1,0:T(8,128)}, u32[]{:S(2)}, u32[]{:S(2)}) async-start(f32[8,64,1024]{2,1,0:T(8,128)} %shard_map.69.refs_5_), calls=%async_computation.1 | async-start | bytes 4194304 | tf_op jit(solution)/shard_map/all_to_all | solution.py:237
  61.9 2.4 %collective-permute-start.16 = (f32[8,16,512]{2,1,0:T(8,128)S(1)}, f32[8,16,512]{2,1,0:T(8,128)S(1)}, u32[]{:S(2)}, u32[]{:S(2)}) collective-permute-start(f32[8,16,512]{2,1,0:T(8,128)S(1)} %get-tuple-element.24.refs_0_), channel_id=1, source_target_pairs={{0,4},{2,6},{4,0},{6,2},{1,5},{3,7},{5,1},{7,3},{8,12},{10,14},{12... | collective-permute-start | bytes 786440 | tf_op jit(solution)/shard_map/ppermute | solution.py:16
  68.2 8.6 %collective-permute-done.15.refs_1_ = f32[8,16,512]{2,1,0:T(8,128)S(1)} collective-permute-done((f32[8,16,512]{2,1,0:T(8,128)S(1)}, f32[8,16,512]{2,1,0:T(8,128)S(1)}, u32[]{:S(2)}, u32[]{:S(2)}) %collective-permute-start.15) | collective-permute-done | bytes 262176 | tf_op jit(solution)/shard_map/ppermute | solution.py:16
  79.5 2.6 %collective-permute-done.12 = f32[64,512]{1,0:T(8,128)S(1)} collective-permute-done((f32[64,512]{1,0:T(8,128)S(1)}, f32[64,512]{1,0:T(8,128)S(1)}, u32[]{:S(2)}, u32[]{:S(2)}) %collective-permute-start.12) | collective-permute-done | bytes 131104 | tf_op jit(solution)/shard_map/ppermute | solution.py:16
  84.4 3.8 %collective-permute-done.14.other = f32[64,512]{1,0:T(8,128)S(1)} collective-permute-done((f32[64,512]{1,0:T(8,128)S(1)}, f32[64,512]{1,0:T(8,128)S(1)}, u32[]{:S(2)}, u32[]{:S(2)}) %collective-permute-start.14) | collective-permute-done | bytes 131104 | tf_op jit(solution)/shard_map/ppermute | solution.py:20
  91.3 2.3 %collective-permute-start.23 = (f32[64,512]{1,0:T(8,128)S(1)}, f32[64,512]{1,0:T(8,128)S(1)}, u32[]{:S(2)}, u32[]{:S(2)}) collective-permute-start(f32[64,512]{1,0:T(8,128)S(1)} %shard_map.73.refs_0_.refs_4_), channel_id=1, source_target_pairs={{0,4},{2,6},{4,0},{6,2},{1,5},{3,7},{5,1},{7,3},{8,12},{10,14},{12... | collective-permute-start | bytes 393224 | tf_op jit(solution)/shard_map/ppermute | solution.py:16
  94.1 2.9 %collective-permute-done.22.refs_1_.refs_5_ = f32[64,512]{1,0:T(8,128)S(1)} collective-permute-done((f32[64,512]{1,0:T(8,128)S(1)}, f32[64,512]{1,0:T(8,128)S(1)}, u32[]{:S(2)}, u32[]{:S(2)}) %collective-permute-start.22) | collective-permute-done | bytes 131104 | tf_op jit(solution)/shard_map/ppermute | solution.py:16
  97.0 2.1 %collective-permute-done.23.refs_2_.refs_6_ = f32[64,512]{1,0:T(8,128)S(1)} collective-permute-done((f32[64,512]{1,0:T(8,128)S(1)}, f32[64,512]{1,0:T(8,128)S(1)}, u32[]{:S(2)}, u32[]{:S(2)}) %collective-permute-start.23) | collective-permute-done | bytes 131104 | tf_op jit(solution)/shard_map/ppermute | solution.py:16
  103.0 2.7 %shard_map.75.refs_8_ = f32[8,80,512]{2,1,0:T(8,128)} custom-call(s32[4]{0:T(128)S(1)} %pad_add_fusion.at, f32[512,128]{1,0:T(8,128)S(1)} %get-tuple-element.16.refs_0_, f32[512,128]{1,0:T(8,128)S(1)} %collective-permute-done.7.refs_1_, f32[512,128]{1,0:T(8,128)S(1)} %collective-permute-done.8.refs_2_, f32[512,128]{1,0:T(8,128)S(1)} %collective-permute-done.9.refs_3_, ...), custom_call_target="tpu_custom_call" | custom-call | tf_op jit(solution)/shard_map/pallas_call | solution.py:256
  105.7 2.2 %collective-permute-done.29.other = f32[256,128]{1,0:T(8,128)S(1)} collective-permute-done((f32[256,128]{1,0:T(8,128)S(1)}, f32[256,128]{1,0:T(8,128)S(1)}, u32[]{:S(2)}, u32[]{:S(2)}) %collective-permute-start.29) | collective-permute-done | bytes 131104 | tf_op jit(solution)/shard_map/ppermute | solution.py:20
  110.0 6.9 %all-to-all-start.2 = ((f32[8,80,512]{2,1,0:T(8,128)}), f32[8,80,512]{2,1,0:T(8,128)S(1)}, u32[]{:S(2)}, u32[]{:S(2)}) async-start(f32[8,80,512]{2,1,0:T(8,128)} %shard_map.76), calls=%async_computation.2 | async-start | bytes 2621440 | tf_op jit(solution)/shard_map/all_to_all | solution.py:267
  118.7 12.6 %collective-permute-done.30 = f32[16,1024]{0,1:T(8,128)} collective-permute-done((f32[16,1024]{0,1:T(8,128)}, f32[16,1024]{0,1:T(8,128)}, u32[]{:S(2)}, u32[]{:S(2)}) %collective-permute-start.30) | collective-permute-done | bytes 65568 | tf_op jit(solution)/shard_map/ppermute | solution.py:20
  131.3 2.2 %fusion.gram = f32[16,512]{1,0:T(8,128)S(1)} fusion(f32[1024,512]{1,0:T(8,128)S(1)} %bitcast.10, f32[16,1024]{0,1:T(8,128)} %dynamic-slice_bitcast_fusion, f32[16,1024]{0,1:T(8,128)} %collective-permute-done.30, pred[]{:T(512)S(6)} %eq.6), kind=kOutput, calls=%fused_computation | convolution fusion | flops 100679680 | bytes 2260993 | tf_op jit(solution)/shard_map/dot_general | solution.py:272
  133.5 2.5 %reduce_sum.9 = f32[64,1024]{1,0:T(8,128)} reduce(f32[8,64,1024]{2,1,0:T(8,128)} %all-to-all-done.1, f32[]{:T(128)} %constant.49.clone.1), dimensions={0}, to_apply=%region_0.1 | reduce | flops 458752 | bytes 2359300 | tf_op jit(solution)/shard_map/reduce_sum | solution.py:276
  135.9 15.0 %all-to-all-done.2.got = f32[8,80,512]{2,1,0:T(8,128)S(1)} async-done(((f32[8,80,512]{2,1,0:T(8,128)}), f32[8,80,512]{2,1,0:T(8,128)S(1)}, u32[]{:S(2)}, u32[]{:S(2)}) %all-to-all-start.2) | async-done | bytes 1310752 | tf_op jit(solution)/shard_map/all_to_all | solution.py:267
  (70 shorter events, 37.4 us)
Async XLA Ops:
  5.1 47.2 %all-to-all-start = ((f32[8,80,512]{2,1,0:T(8,128)}), f32[8,80,512]{2,1,0:T(8,128)S(1)}, u32[]{:S(2)}, u32[]{:S(2)}) async-start(f32[8,80,512]{2,1,0:T(8,128)} %shard_map.68), calls=%async_computation | async-start | bytes 2621440 | tf_op jit(solution)/shard_map/all_to_all | solution.py:228
  13.5 9.5 %collective-permute-start = (f32[64,1024]{1,0:T(8,128)S(1)}, f32[64,1024]{1,0:T(8,128)S(1)}, u32[]{:S(2)}, u32[]{:S(2)}) collective-permute-start(f32[64,1024]{1,0:T(8,128)S(1)} %copy-done), channel_id=1, source_target_pairs={{0,2},{2,4},{4,6},{6,0},{1,3},{3,5},{5,7},{7,1},{8,10},{10,12},{12... | collective-permute-start | bytes 786440 | tf_op jit(solution)/shard_map/ppermute | solution.py:16
  15.1 14.1 %collective-permute-start.1 = (f32[64,1024]{1,0:T(8,128)S(1)}, f32[64,1024]{1,0:T(8,128)S(1)}, u32[]{:S(2)}, u32[]{:S(2)}) collective-permute-start(f32[64,1024]{1,0:T(8,128)S(1)} %copy-done), channel_id=1, source_target_pairs={{0,4},{2,6},{4,0},{6,2},{1,5},{3,7},{5,1},{7,3},{8,12},{10,14},{12... | collective-permute-start | bytes 786440 | tf_op jit(solution)/shard_map/ppermute | solution.py:16
  17.8 11.4 %collective-permute-start.2 = (f32[64,1024]{1,0:T(8,128)S(1)}, f32[64,1024]{1,0:T(8,128)S(1)}, u32[]{:S(2)}, u32[]{:S(2)}) collective-permute-start(f32[64,1024]{1,0:T(8,128)S(1)} %copy-done), channel_id=1, source_target_pairs={{0,6},{2,0},{4,2},{6,4},{1,7},{3,1},{5,3},{7,5},{8,14},{10,8},{12,... | collective-permute-start | bytes 786440 | tf_op jit(solution)/shard_map/ppermute | solution.py:16
  19.3 10.4 %collective-permute-start.3 = (f32[64,1024]{1,0:T(8,128)S(1)}, f32[64,1024]{1,0:T(8,128)S(1)}, u32[]{:S(2)}, u32[]{:S(2)}) collective-permute-start(f32[64,1024]{1,0:T(8,128)S(1)} %copy-done), channel_id=1, source_target_pairs={{0,1},{1,0},{2,3},{3,2},{4,5},{5,4},{6,7},{7,6},{8,9},{9,8},{10,11... | collective-permute-start | bytes 786440 | tf_op jit(solution)/shard_map/ppermute | solution.py:20
  23.1 6.6 %collective-permute-start.4 = (f32[64,1024]{1,0:T(8,128)S(1)}, f32[64,1024]{1,0:T(8,128)S(1)}, u32[]{:S(2)}, u32[]{:S(2)}) collective-permute-start(f32[64,1024]{1,0:T(8,128)S(1)} %collective-permute-done.refs_1_), channel_id=1, source_target_pairs={{0,1},{1,0},{2,3},{3,2},{4,5},{5,4},{6,7},{7,6},{8,9},{9,8},{10,11... | collective-permute-start | bytes 786440 | tf_op jit(solution)/shard_map/ppermute | solution.py:20
  32.4 9.2 %collective-permute-start.7 = (f32[512,128]{1,0:T(8,128)S(1)}, f32[512,128]{1,0:T(8,128)S(1)}, u32[]{:S(2)}, u32[]{:S(2)}) collective-permute-start(f32[512,128]{1,0:T(8,128)S(1)} %get-tuple-element.16.refs_0_), channel_id=1, source_target_pairs={{0,64},{64,128},{128,192},{192,0},{1,65},{65,129},{129,193},{193,1... | collective-permute-start | bytes 786440 | tf_op jit(solution)/shard_map/ppermute | solution.py:16
  34.0 10.7 %collective-permute-start.8 = (f32[512,128]{1,0:T(8,128)S(1)}, f32[512,128]{1,0:T(8,128)S(1)}, u32[]{:S(2)}, u32[]{:S(2)}) collective-permute-start(f32[512,128]{1,0:T(8,128)S(1)} %get-tuple-element.16.refs_0_), channel_id=1, source_target_pairs={{0,128},{64,192},{128,0},{192,64},{1,129},{65,193},{129,1},{193,65... | collective-permute-start | bytes 786440 | tf_op jit(solution)/shard_map/ppermute | solution.py:16
  35.0 13.6 %collective-permute-start.9 = (f32[512,128]{1,0:T(8,128)S(1)}, f32[512,128]{1,0:T(8,128)S(1)}, u32[]{:S(2)}, u32[]{:S(2)}) collective-permute-start(f32[512,128]{1,0:T(8,128)S(1)} %get-tuple-element.16.refs_0_), channel_id=1, source_target_pairs={{0,192},{64,0},{128,64},{192,128},{1,193},{65,1},{129,65},{193,129... | collective-permute-start | bytes 786440 | tf_op jit(solution)/shard_map/ppermute | solution.py:16
  52.3 57.7 %all-to-all-start.1 = ((f32[8,64,1024]{2,1,0:T(8,128)}), f32[8,64,1024]{2,1,0:T(8,128)}, u32[]{:S(2)}, u32[]{:S(2)}) async-start(f32[8,64,1024]{2,1,0:T(8,128)} %shard_map.69.refs_5_), calls=%async_computation.1 | async-start | bytes 4194304 | tf_op jit(solution)/shard_map/all_to_all | solution.py:237
  60.9 15.9 %collective-permute-start.15 = (f32[8,16,512]{2,1,0:T(8,128)S(1)}, f32[8,16,512]{2,1,0:T(8,128)S(1)}, u32[]{:S(2)}, u32[]{:S(2)}) collective-permute-start(f32[8,16,512]{2,1,0:T(8,128)S(1)} %get-tuple-element.24.refs_0_), channel_id=1, source_target_pairs={{0,2},{2,4},{4,6},{6,0},{1,3},{3,5},{5,7},{7,1},{8,10},{10,12},{12... | collective-permute-start | bytes 786440 | tf_op jit(solution)/shard_map/ppermute | solution.py:16
  61.9 15.1 %collective-permute-start.16 = (f32[8,16,512]{2,1,0:T(8,128)S(1)}, f32[8,16,512]{2,1,0:T(8,128)S(1)}, u32[]{:S(2)}, u32[]{:S(2)}) collective-permute-start(f32[8,16,512]{2,1,0:T(8,128)S(1)} %get-tuple-element.24.refs_0_), channel_id=1, source_target_pairs={{0,4},{2,6},{4,0},{6,2},{1,5},{3,7},{5,1},{7,3},{8,12},{10,14},{12... | collective-permute-start | bytes 786440 | tf_op jit(solution)/shard_map/ppermute | solution.py:16
  64.3 13.5 %collective-permute-start.17 = (f32[8,16,512]{2,1,0:T(8,128)S(1)}, f32[8,16,512]{2,1,0:T(8,128)S(1)}, u32[]{:S(2)}, u32[]{:S(2)}) collective-permute-start(f32[8,16,512]{2,1,0:T(8,128)S(1)} %get-tuple-element.24.refs_0_), channel_id=1, source_target_pairs={{0,6},{2,0},{4,2},{6,4},{1,7},{3,1},{5,3},{7,5},{8,14},{10,8},{12,... | collective-permute-start | bytes 786440 | tf_op jit(solution)/shard_map/ppermute | solution.py:16
  66.5 13.1 %collective-permute-start.13 = (f32[64,512]{1,0:T(8,128)S(1)}, f32[64,512]{1,0:T(8,128)S(1)}, u32[]{:S(2)}, u32[]{:S(2)}) collective-permute-start(f32[64,512]{1,0:T(8,128)S(1)} %get-tuple-element.23), channel_id=1, source_target_pairs={{0,2},{2,4},{4,6},{6,0},{1,3},{3,5},{5,7},{7,1},{8,10},{10,12},{12... | collective-permute-start | bytes 393224 | tf_op jit(solution)/shard_map/ppermute | solution.py:16
  67.0 15.2 %collective-permute-start.12 = (f32[64,512]{1,0:T(8,128)S(1)}, f32[64,512]{1,0:T(8,128)S(1)}, u32[]{:S(2)}, u32[]{:S(2)}) collective-permute-start(f32[64,512]{1,0:T(8,128)S(1)} %get-tuple-element.22), channel_id=1, source_target_pairs={{0,4},{2,6},{4,0},{6,2},{1,5},{3,7},{5,1},{7,3},{8,12},{10,14},{12... | collective-permute-start | bytes 393224 | tf_op jit(solution)/shard_map/ppermute | solution.py:16
  76.7 6.0 %collective-permute-start.11 = (f32[64,512]{1,0:T(8,128)S(1)}, f32[64,512]{1,0:T(8,128)S(1)}, u32[]{:S(2)}, u32[]{:S(2)}) collective-permute-start(f32[64,512]{1,0:T(8,128)S(1)} %get-tuple-element.21), channel_id=1, source_target_pairs={{0,6},{2,0},{4,2},{6,4},{1,7},{3,1},{5,3},{7,5},{8,14},{10,8},{12,... | collective-permute-start | bytes 393224 | tf_op jit(solution)/shard_map/ppermute | solution.py:16
  77.0 6.6 %collective-permute-start.18 = (f32[8,16,512]{2,1,0:T(8,128)S(1)}, f32[8,16,512]{2,1,0:T(8,128)S(1)}, u32[]{:S(2)}, u32[]{:S(2)}) collective-permute-start(f32[8,16,512]{2,1,0:T(8,128)S(1)} %get-tuple-element.24.refs_0_), channel_id=1, source_target_pairs={{0,1},{1,0},{2,3},{3,2},{4,5},{5,4},{6,7},{7,6},{8,9},{9,8},{10,11... | collective-permute-start | bytes 786440 | tf_op jit(solution)/shard_map/ppermute | solution.py:20
  77.8 5.8 %collective-permute-start.19 = (f32[8,16,512]{2,1,0:T(8,128)S(1)}, f32[8,16,512]{2,1,0:T(8,128)S(1)}, u32[]{:S(2)}, u32[]{:S(2)}) collective-permute-start(f32[8,16,512]{2,1,0:T(8,128)S(1)} %collective-permute-done.15.refs_1_), channel_id=1, source_target_pairs={{0,1},{1,0},{2,3},{3,2},{4,5},{5,4},{6,7},{7,6},{8,9},{9,8},{10,11... | collective-permute-start | bytes 786440 | tf_op jit(solution)/shard_map/ppermute | solution.py:20
  89.5 7.5 %collective-permute-start.22 = (f32[64,512]{1,0:T(8,128)S(1)}, f32[64,512]{1,0:T(8,128)S(1)}, u32[]{:S(2)}, u32[]{:S(2)}) collective-permute-start(f32[64,512]{1,0:T(8,128)S(1)} %shard_map.73.refs_0_.refs_4_), channel_id=1, source_target_pairs={{0,2},{2,4},{4,6},{6,0},{1,3},{3,5},{5,7},{7,1},{8,10},{10,12},{12... | collective-permute-start | bytes 393224 | tf_op jit(solution)/shard_map/ppermute | solution.py:16
  91.3 7.8 %collective-permute-start.23 = (f32[64,512]{1,0:T(8,128)S(1)}, f32[64,512]{1,0:T(8,128)S(1)}, u32[]{:S(2)}, u32[]{:S(2)}) collective-permute-start(f32[64,512]{1,0:T(8,128)S(1)} %shard_map.73.refs_0_.refs_4_), channel_id=1, source_target_pairs={{0,4},{2,6},{4,0},{6,2},{1,5},{3,7},{5,1},{7,3},{8,12},{10,14},{12... | collective-permute-start | bytes 393224 | tf_op jit(solution)/shard_map/ppermute | solution.py:16
  94.1 5.5 %collective-permute-start.25 = (f32[64,512]{1,0:T(8,128)S(1)}, f32[64,512]{1,0:T(8,128)S(1)}, u32[]{:S(2)}, u32[]{:S(2)}) collective-permute-start(f32[64,512]{1,0:T(8,128)S(1)} %shard_map.73.refs_0_.refs_4_), channel_id=1, source_target_pairs={{0,1},{1,0},{2,3},{3,2},{4,5},{5,4},{6,7},{7,6},{8,9},{9,8},{10,11... | collective-permute-start | bytes 393224 | tf_op jit(solution)/shard_map/ppermute | solution.py:20
  101.9 6.0 %collective-permute-start.29 = (f32[256,128]{1,0:T(8,128)S(1)}, f32[256,128]{1,0:T(8,128)S(1)}, u32[]{:S(2)}, u32[]{:S(2)}) collective-permute-start(f32[256,128]{1,0:T(8,128)S(1)} %shard_map.74.own), channel_id=1, source_target_pairs={{0,64},{64,0},{128,192},{192,128},{1,65},{65,1},{129,193},{193,129... | collective-permute-start | bytes 393224 | tf_op jit(solution)/shard_map/ppermute | solution.py:20
  110.0 41.0 %all-to-all-start.2 = ((f32[8,80,512]{2,1,0:T(8,128)}), f32[8,80,512]{2,1,0:T(8,128)S(1)}, u32[]{:S(2)}, u32[]{:S(2)}) async-start(f32[8,80,512]{2,1,0:T(8,128)} %shard_map.76), calls=%async_computation.2 | async-start | bytes 2621440 | tf_op jit(solution)/shard_map/all_to_all | solution.py:267
  117.9 13.4 %collective-permute-start.30 = (f32[16,1024]{0,1:T(8,128)}, f32[16,1024]{0,1:T(8,128)}, u32[]{:S(2)}, u32[]{:S(2)}) collective-permute-start(f32[16,1024]{0,1:T(8,128)} %dynamic-slice_bitcast_fusion), channel_id=1, source_target_pairs={{0,64},{64,0},{128,192},{192,128},{1,65},{65,1},{129,193},{193,129... | collective-permute-start | bytes 196616 | tf_op jit(solution)/shard_map/ppermute | solution.py:20
  (15 other events, 78.1 us)

commit v3 on v2

--- a/solution.py
+++ b/solution.py
@@ -66,24 +66,8 @@
     return below + jnp.where(cols == rows, 1.0, 0.0).astype(F32)
 
 
-def row_mask(at, pattern, rows):
-    block = (at[1] * NXC + at[2] * NC + at[3]) * rows // BLK
-    return pattern[at[0] // 2, block].astype(F32)
-
-
-def stack_rows(at, pattern, level, coupling, after, stacks, nodes, rows_in, sem):
-    del after
-    moves = [pltpu.make_async_copy(level, nodes, sem.at[0]), pltpu.make_async_copy(coupling, rows_in, sem.at[1])]
-    for move in moves:
-        move.start()
-    for move in moves:
-        move.wait()
-    rows, g = coupling.shape[0], at[1] * NXC + at[2] * NC + at[3]
-    masked = rows_in[...] * row_mask(at, pattern, rows)
-    low = lower_piece(nodes[...], g * level.shape[0], at[0] % 2 * level.shape[1])
-    for to in range(NZ):
-        stacks[to, :rows] = masked
-        stacks[to, rows:] = low
+def row_mask(at, z, pattern, rows):
+    return pattern[at[0] // 2, (z * NXC + at[2] * NC + at[3]) * rows // BLK].astype(F32)
 
 
 def root_columns(at, *refs):
@@ -113,14 +97,19 @@
         out[pl.ds(pl.multiple_of((chip * NC + core) * rows, rows), rows)] = block[...]
 
 
-def mix(at, *refs):
-    columns, stacks, (keep, give, nodes, full, part) = refs[:NY], refs[NY], refs[NY + 2:]
+def take_nodes(at, stacks, nodes, sem):
+    move = pltpu.make_async_copy(stacks.at[:, stacks.shape[1] - nodes.shape[1]:], nodes, sem.at[0])
+    move.start()
+    move.wait()
+
+
+def mix(at, pattern, *refs):
+    columns, stacks, (keep, give, full, part) = refs[:NY], refs[NY], refs[NY + 2:]
     rows, per_y = keep.shape[1], NZ // NY
     for s in range(NY):
         k = lax.rem(at[0] + NY - s, NY) * per_y
         for b in range(per_y):
-            full[(s * per_y + b) * rows:(s * per_y + b + 1) * rows] = stacks[k + b, :rows]
-    nodes[...] = stacks[:, rows:]
+            full[(s * per_y + b) * rows:(s * per_y + b + 1) * rows] = stacks[k + b, :rows] * row_mask(at, k + b, pattern, rows)
     part[...] = product(whole_lower(columns), full[...], ROWS)
     for s in range(NX):
         chip = lax.rem(at[2] + NX - s, NX)
@@ -138,8 +127,10 @@
     for k, block in enumerate(blocks):
         s, core = k % NX, at[3] if k < NX else 1 - at[3]
         chip = lax.rem(at[2] + NX - s, NX)
+        count, width = block.shape[1:]
         for b in range(NZ):
-            out[b, chip * NC + core] = block[b]
+            place = chip * NC + core
+            out[b, place] = lower_piece(block[b], (b * NXC + place) * count, at[0] % 2 * width)
 
 
 def solve(at, own, other, node, out):
@@ -159,9 +150,27 @@
             out[k + b, :rows] = value[at_row:at_row + rows]
 
 
+def root_part(at, first, columns, whole, out, part, sem):
+    rows, per_y = out.shape[1], NZ // NY
+    part[...] = product(whole_lower(columns), whole[...], COLS)
+    moves = []
+    for s in range(len(columns)):
+        k = lax.rem(at[0] + NY - s - first, NY) * per_y
+        for b in range(per_y):
+            from_rows = part.at[pl.ds((s * per_y + b) * rows, rows)]
+            moves.append(pltpu.make_async_copy(from_rows, out.at[k + b], sem.at[len(moves)]))
+            moves[-1].start()
+    for move in moves:
+        move.wait()
+
+
 def root_product(at, *refs):
-    columns, (whole, out) = refs[:NY], refs[NY:]
-    store_by_y(at, product(whole_lower(columns), whole[...], COLS), out, out.shape[1])
+    root_part(at, 0, refs[:NY // 2], *refs[NY // 2:])
+
+
+def root_rest(at, *refs):
+    columns, whole, _, out, part, sem = refs[:NY // 2], *refs[NY // 2:]
+    root_part(at, NY // 2, columns, whole, out, part, sem)
 
 
 def choose(at, *refs):
@@ -203,7 +212,7 @@
     for k in range(1, NZ):
         total = total + got[k]
     rows = cross.shape[0]
-    cross[...] = -(total[:rows] * row_mask(at, pattern, rows))
+    cross[...] = -(total[:rows] * row_mask(at, at[1], pattern, rows))
     node[...] = gram[...] + total[rows:]
 
 
@@ -216,38 +225,45 @@
     at = jnp.stack([y, z, x, c]).astype(jnp.int32)
     per = rows + node_rows
     smem, vmem, anywhere = (pl.BlockSpec(memory_space=m) for m in (pltpu.SMEM, pltpu.VMEM, pl.ANY))
+    outside = pl.BlockSpec(memory_space=pltpu.HBM)
 
     blocks = chip_blocks(root_inverse)
-    stacks = call(
-        stack_rows,
-        [(NZ, per, width)],
-        [(node_rows, width), (rows, width)],
-        in_specs=[smem, smem, anywhere, anywhere, anywhere],
-        copies=2,
-    )(at, pattern, level_inverse, coupling, level_inverse)[0]
+    stacks = jnp.broadcast_to(jnp.concatenate([coupling, level_inverse])[None], (NZ, per, width))
     stacks = lax.all_to_all(stacks, "z", 0, 0, tiled=True)
+    nodes = call(take_nodes, [(NZ, node_rows, width)], in_specs=[smem, anywhere], copies=1)(at, stacks)[0]
+    nodes = chip_blocks(nodes)
     whole, columns = call(root_columns, [(NXC * rows, cols), (NXC * rows, cols // NXC)], n_in=NXC)(
         at, *blocks
     )
     columns = [columns] + [shifted(columns, "y", s) for s in range(1, NY)]
 
-    root = call(root_product, [(NZ, rows, cols)], n_in=NY + 1)(
-        at, *columns, whole
-    )[0]
+    shape, part = [(NZ, rows, cols)], [(NZ // 2 * rows, cols)]
+    root = call(
+        root_product, shape, part, NY // 2 + 1, out_specs=[outside], copies=NZ // 2
+    )(at, *columns[:NY // 2], whole)[0]
+    root = call(
+        root_rest,
+        shape,
+        part,
+        in_specs=[smem] + [vmem] * (NY // 2 + 1) + [outside],
+        out_specs=[outside],
+        aliases={NY // 2 + 2: 0},
+        copies=NZ // 2,
+    )(at, *columns[NY // 2:], whole, root)[0]
     summed = lax.all_to_all(root, "z", 0, 0, tiled=True)
 
-    keep, give, nodes = call(
+    keep, give = call(
         mix,
-        [(NX, rows, width), (NX, rows, width), (NZ, node_rows, width)],
+        [(NX, rows, width)] * 2,
         [(NZ * rows, width), (NXC * rows, width)],
-        in_specs=[smem] + [vmem] * (NY + 1) + [anywhere],
-    )(at, *columns, stacks, root)
+        in_specs=[smem, smem] + [vmem] * (NY + 1) + [anywhere],
+    )(at, pattern, *columns, stacks, root)
     parts = call(add_cores, [(rows, width)] * NX, n_in=2)(at, keep, from_partner(give, "c"))
     mixed = parts[0]
     for s in range(1, NX):
         mixed = mixed + shifted(parts[s], "x", -s)
 
-    node_all = call(whole_node, [(NZ, NXC, node_rows, width)], n_in=NXC)(at, *chip_blocks(nodes))[0]
+    node_all = call(whole_node, [(NZ, NXC, node_rows, width)], n_in=NXC)(at, *nodes)[0]
     node_all = node_all.reshape(NZ * NXC * node_rows, width)
     solved = call(solve, [(rows, width)], n_in=3)(at, mixed, from_partner(mixed, "y"), node_all)[0]
     solved = chip_blocks(solved)

time: 154 us -> 153 us (level)
  waiting for transfers between devices: 77.2 us -> 73.9 us
    ppermute x15, waiting for transfers between devices: 40.7 us -> 38 us  [shifted(): lax.ppermute(value, axis, [(i, (i + step) % size) for i in range(size)])]
    pallas_call x4 -> x5, Pallas kernels: 8.02 us -> 8.48 us  [the longest x1 2.69 us: on_device(): call(root_product, shape, part, NY // 2 + 1, out_specs=[outside], copies=...]
  transfers between devices with their start and end apart: 34 -> 34, of which waited for: 24 -> 23; matrix products, arithmetic and copies ran while one was open for 4% -> 4% of each run, Pallas kernels for 10% -> 11%
where the time goes in v3:
time: 153 us; the launch traced here: 151 us
  waiting for transfers between devices  73.9 us (48%)
  starting transfers between devices  48.4 us (32%)
  Pallas kernels  18.6 us (12%)
  local copies, waits for them, and re-layouts  3.94 us (3%)
  other arithmetic  3.5 us (2%)
  matrix products  2.18 us (1%)
    ppermute x15, waiting for transfers between devices, shifted(): lax.ppermute(value, axis, [(i, (i + step) % size) for i in range(size)])  38 us
    ppermute x15, starting transfers between devices, shifted(): lax.ppermute(value, axis, [(i, (i + step) % size) for i in range(size)])  22 us
    ppermute x16, waiting for transfers between devices, from_partner(): lax.ppermute(value, axis, [(i, i ^ 1) for i in range(lax.axis_size(axis))])  20.8 us
    all_to_all x1, waiting for transfers between devices, on_device(): both = lax.all_to_all(both, 'z', 0, 0, tiled=True)  15 us
    all_to_all x1, starting transfers between devices, on_device(): stacks = lax.all_to_all(stacks, 'z', 0, 0, tiled=True)  8.47 us
    all_to_all x1, starting transfers between devices, on_device(): both = lax.all_to_all(both, 'z', 0, 0, tiled=True)  7.2 us
    all_to_all x1, starting transfers between devices, on_device(): summed = lax.all_to_all(root, 'z', 0, 0, tiled=True)  6.86 us
    ppermute x16, starting transfers between devices, from_partner(): lax.ppermute(value, axis, [(i, i ^ 1) for i in range(lax.axis_size(axis))])  3.87 us
  transfers between devices with their start and end apart: 34, of which 23 were waited for; matrix products, arithmetic and copies ran while one was open for 4% of the time, Pallas kernels for 11%

profile of v3, /device:TPU:8, one launch (start us, length us, event | category | flops | bytes accessed | tf_op | source)
XLA Modules:
  0.0 151.3 jit_solution(8010318244989088819)
XLA Ops:
  2.9 8.5 %all-to-all-start = ((f32[8,80,512]{2,1,0:T(8,128)}), f32[8,80,512]{2,1,0:T(8,128)S(1)}, u32[]{:S(2)}, u32[]{:S(2)}) async-start(f32[8,80,512]{2,1,0:T(8,128)} %broadcast_in_dim.2), calls=%async_computation | async-start | bytes 2621440 | tf_op jit(solution)/shard_map/all_to_all | solution.py:232
  12.9 2.7 %collective-permute-start.1 = (f32[64,1024]{1,0:T(8,128)S(1)}, f32[64,1024]{1,0:T(8,128)S(1)}, u32[]{:S(2)}, u32[]{:S(2)}) collective-permute-start(f32[64,1024]{1,0:T(8,128)S(1)} %copy-done), channel_id=1, source_target_pairs={{0,4},{2,6},{4,0},{6,2},{1,5},{3,7},{5,1},{7,3},{8,12},{10,14},{12... | collective-permute-start | bytes 786440 | tf_op jit(solution)/shard_map/ppermute | solution.py:16
  17.1 3.8 %collective-permute-done.refs_1_ = f32[64,1024]{1,0:T(8,128)S(1)} collective-permute-done((f32[64,1024]{1,0:T(8,128)S(1)}, f32[64,1024]{1,0:T(8,128)S(1)}, u32[]{:S(2)}, u32[]{:S(2)}) %collective-permute-start) | collective-permute-done | bytes 262176 | tf_op jit(solution)/shard_map/ppermute | solution.py:16
  20.9 6.1 %collective-permute-done.1.refs_2_ = f32[64,1024]{1,0:T(8,128)S(1)} collective-permute-done((f32[64,1024]{1,0:T(8,128)S(1)}, f32[64,1024]{1,0:T(8,128)S(1)}, u32[]{:S(2)}, u32[]{:S(2)}) %collective-permute-start.1) | collective-permute-done | bytes 262176 | tf_op jit(solution)/shard_map/ppermute | solution.py:16
  34.4 2.4 %collective-permute-start.9 = (f32[512,128]{1,0:T(8,128)S(1)}, f32[512,128]{1,0:T(8,128)S(1)}, u32[]{:S(2)}, u32[]{:S(2)}) collective-permute-start(f32[512,128]{1,0:T(8,128)S(1)} %get-tuple-element.15.refs_0_), channel_id=1, source_target_pairs={{0,192},{64,0},{128,64},{192,128},{1,193},{65,1},{129,65},{193,129... | collective-permute-start | bytes 786440 | tf_op jit(solution)/shard_map/ppermute | solution.py:16
  36.8 4.2 %collective-permute-done.7.refs_1_ = f32[512,128]{1,0:T(8,128)S(1)} collective-permute-done((f32[512,128]{1,0:T(8,128)S(1)}, f32[512,128]{1,0:T(8,128)S(1)}, u32[]{:S(2)}, u32[]{:S(2)}) %collective-permute-start.7) | collective-permute-done | bytes 262176 | tf_op jit(solution)/shard_map/ppermute | solution.py:16
  41.0 2.7 %shard_map.68.refs_3_ = f32[8,64,1024]{2,1,0:T(8,128)} custom-call(s32[4]{0:T(128)S(1)} %pad_add_fusion.at, f32[512,128]{1,0:T(8,128)S(1)} %get-tuple-element.15.refs_0_, f32[512,128]{1,0:T(8,128)S(1)} %collective-permute-done.7.refs_1_, f32[512,1024]{1,0:T(8,128)S(1)} %get-tuple-element.16.refs_2_), custom_call_target="tpu_custom_call" | custom-call | tf_op jit(solution)/shard_map/pallas_call | solution.py:241
  44.2 3.8 %collective-permute-done.9.refs_1_.refs_3_ = f32[512,128]{1,0:T(8,128)S(1)} collective-permute-done((f32[512,128]{1,0:T(8,128)S(1)}, f32[512,128]{1,0:T(8,128)S(1)}, u32[]{:S(2)}, u32[]{:S(2)}) %collective-permute-start.9) | collective-permute-done | bytes 262176 | tf_op jit(solution)/shard_map/ppermute | solution.py:16
  48.0 2.7 %shard_map.69.refs_5_ = f32[8,64,1024]{2,1,0:T(8,128)} custom-call(s32[4]{0:T(128)S(1)} %pad_add_fusion.at, f32[512,128]{1,0:T(8,128)S(1)} %collective-permute-done.8.refs_0_.refs_2_, f32[512,128]{1,0:T(8,128)S(1)} %collective-permute-done.9.refs_1_.refs_3_, f32[512,1024]{1,0:T(8,128)S(1)} %get-tuple-element.16.refs_2_, ...), custom_call_target="tpu_custom_call", output_to_operand_aliasing={{}: (4, {})} | custom-call | tf_op jit(solution)/shard_map/pallas_call | solution.py:244
  50.7 6.9 %all-to-all-start.1 = ((f32[8,64,1024]{2,1,0:T(8,128)}), f32[8,64,1024]{2,1,0:T(8,128)}, u32[]{:S(2)}, u32[]{:S(2)}) async-start(f32[8,64,1024]{2,1,0:T(8,128)} %shard_map.69.refs_5_), calls=%async_computation.1 | async-start | bytes 4194304 | tf_op jit(solution)/shard_map/all_to_all | solution.py:253
  60.9 2.4 %collective-permute-start.16 = (f32[8,16,512]{2,1,0:T(8,128)S(1)}, f32[8,16,512]{2,1,0:T(8,128)S(1)}, u32[]{:S(2)}, u32[]{:S(2)}) collective-permute-start(f32[8,16,512]{2,1,0:T(8,128)S(1)} %shard_map.72.refs_0_), channel_id=1, source_target_pairs={{0,4},{2,6},{4,0},{6,2},{1,5},{3,7},{5,1},{7,3},{8,12},{10,14},{12... | collective-permute-start | bytes 786440 | tf_op jit(solution)/shard_map/ppermute | solution.py:16
  67.1 8.6 %collective-permute-done.15.refs_1_ = f32[8,16,512]{2,1,0:T(8,128)S(1)} collective-permute-done((f32[8,16,512]{2,1,0:T(8,128)S(1)}, f32[8,16,512]{2,1,0:T(8,128)S(1)}, u32[]{:S(2)}, u32[]{:S(2)}) %collective-permute-start.15) | collective-permute-done | bytes 262176 | tf_op jit(solution)/shard_map/ppermute | solution.py:16
  78.5 2.7 %collective-permute-done.12 = f32[64,512]{1,0:T(8,128)S(1)} collective-permute-done((f32[64,512]{1,0:T(8,128)S(1)}, f32[64,512]{1,0:T(8,128)S(1)}, u32[]{:S(2)}, u32[]{:S(2)}) %collective-permute-start.12) | collective-permute-done | bytes 131104 | tf_op jit(solution)/shard_map/ppermute | solution.py:16
  83.7 3.6 %collective-permute-done.14.other = f32[64,512]{1,0:T(8,128)S(1)} collective-permute-done((f32[64,512]{1,0:T(8,128)S(1)}, f32[64,512]{1,0:T(8,128)S(1)}, u32[]{:S(2)}, u32[]{:S(2)}) %collective-permute-start.14) | collective-permute-done | bytes 131104 | tf_op jit(solution)/shard_map/ppermute | solution.py:20
  90.3 2.3 %collective-permute-start.23 = (f32[64,512]{1,0:T(8,128)S(1)}, f32[64,512]{1,0:T(8,128)S(1)}, u32[]{:S(2)}, u32[]{:S(2)}) collective-permute-start(f32[64,512]{1,0:T(8,128)S(1)} %shard_map.74.refs_0_.refs_4_), channel_id=1, source_target_pairs={{0,4},{2,6},{4,0},{6,2},{1,5},{3,7},{5,1},{7,3},{8,12},{10,14},{12... | collective-permute-start | bytes 393224 | tf_op jit(solution)/shard_map/ppermute | solution.py:16
  93.1 2.9 %collective-permute-done.22.refs_1_.refs_5_ = f32[64,512]{1,0:T(8,128)S(1)} collective-permute-done((f32[64,512]{1,0:T(8,128)S(1)}, f32[64,512]{1,0:T(8,128)S(1)}, u32[]{:S(2)}, u32[]{:S(2)}) %collective-permute-start.22) | collective-permute-done | bytes 131104 | tf_op jit(solution)/shard_map/ppermute | solution.py:16
  96.0 2.1 %collective-permute-done.23.refs_2_.refs_6_ = f32[64,512]{1,0:T(8,128)S(1)} collective-permute-done((f32[64,512]{1,0:T(8,128)S(1)}, f32[64,512]{1,0:T(8,128)S(1)}, u32[]{:S(2)}, u32[]{:S(2)}) %collective-permute-start.23) | collective-permute-done | bytes 131104 | tf_op jit(solution)/shard_map/ppermute | solution.py:16
  102.0 2.7 %shard_map.76.refs_8_ = f32[8,80,512]{2,1,0:T(8,128)} custom-call(s32[4]{0:T(128)S(1)} %pad_add_fusion.at, f32[512,128]{1,0:T(8,128)S(1)} %get-tuple-element.15.refs_0_, f32[512,128]{1,0:T(8,128)S(1)} %collective-permute-done.7.refs_1_, f32[512,128]{1,0:T(8,128)S(1)} %collective-permute-done.8.refs_0_.refs_2_, ...), custom_call_target="tpu_custom_call" | custom-call | tf_op jit(solution)/shard_map/pallas_call | solution.py:272
  104.7 2.2 %collective-permute-done.29.other = f32[256,128]{1,0:T(8,128)S(1)} collective-permute-done((f32[256,128]{1,0:T(8,128)S(1)}, f32[256,128]{1,0:T(8,128)S(1)}, u32[]{:S(2)}, u32[]{:S(2)}) %collective-permute-start.29) | collective-permute-done | bytes 131104 | tf_op jit(solution)/shard_map/ppermute | solution.py:20
  108.8 7.2 %all-to-all-start.2 = ((f32[8,80,512]{2,1,0:T(8,128)}), f32[8,80,512]{2,1,0:T(8,128)S(1)}, u32[]{:S(2)}, u32[]{:S(2)}) async-start(f32[8,80,512]{2,1,0:T(8,128)} %shard_map.77), calls=%async_computation.2 | async-start | bytes 2621440 | tf_op jit(solution)/shard_map/all_to_all | solution.py:283
  117.8 12.6 %collective-permute-done.30 = f32[16,1024]{0,1:T(8,128)} collective-permute-done((f32[16,1024]{0,1:T(8,128)}, f32[16,1024]{0,1:T(8,128)}, u32[]{:S(2)}, u32[]{:S(2)}) %collective-permute-start.30) | collective-permute-done | bytes 65568 | tf_op jit(solution)/shard_map/ppermute | solution.py:20
  130.4 2.2 %fusion.gram = f32[16,512]{1,0:T(8,128)S(1)} fusion(f32[1024,512]{1,0:T(8,128)S(1)} %bitcast.10, f32[16,1024]{0,1:T(8,128)} %dynamic-slice_bitcast_fusion, f32[16,1024]{0,1:T(8,128)} %collective-permute-done.30, pred[]{:T(512)S(6)} %eq.6), kind=kOutput, calls=%fused_computation | convolution fusion | flops 100679680 | bytes 2260993 | tf_op jit(solution)/shard_map/dot_general | solution.py:288
  132.5 2.5 %reduce_sum.9 = f32[64,1024]{1,0:T(8,128)} reduce(f32[8,64,1024]{2,1,0:T(8,128)} %all-to-all-done.1, f32[]{:T(128)} %constant.49.clone.1), dimensions={0}, to_apply=%region_0.1 | reduce | flops 458752 | bytes 2359300 | tf_op jit(solution)/shard_map/reduce_sum | solution.py:292
  135.0 15.0 %all-to-all-done.2.got = f32[8,80,512]{2,1,0:T(8,128)S(1)} async-done(((f32[8,80,512]{2,1,0:T(8,128)}), f32[8,80,512]{2,1,0:T(8,128)S(1)}, u32[]{:S(2)}, u32[]{:S(2)}) %all-to-all-start.2) | async-done | bytes 1310752 | tf_op jit(solution)/shard_map/all_to_all | solution.py:283
  (71 shorter events, 37.8 us)
Async XLA Ops:
  2.9 47.8 %all-to-all-start = ((f32[8,80,512]{2,1,0:T(8,128)}), f32[8,80,512]{2,1,0:T(8,128)S(1)}, u32[]{:S(2)}, u32[]{:S(2)}) async-start(f32[8,80,512]{2,1,0:T(8,128)} %broadcast_in_dim.2), calls=%async_computation | async-start | bytes 2621440 | tf_op jit(solution)/shard_map/all_to_all | solution.py:232
  11.3 9.5 %collective-permute-start = (f32[64,1024]{1,0:T(8,128)S(1)}, f32[64,1024]{1,0:T(8,128)S(1)}, u32[]{:S(2)}, u32[]{:S(2)}) collective-permute-start(f32[64,1024]{1,0:T(8,128)S(1)} %copy-done), channel_id=1, source_target_pairs={{0,2},{2,4},{4,6},{6,0},{1,3},{3,5},{5,7},{7,1},{8,10},{10,12},{12... | collective-permute-start | bytes 786440 | tf_op jit(solution)/shard_map/ppermute | solution.py:16
  12.9 14.1 %collective-permute-start.1 = (f32[64,1024]{1,0:T(8,128)S(1)}, f32[64,1024]{1,0:T(8,128)S(1)}, u32[]{:S(2)}, u32[]{:S(2)}) collective-permute-start(f32[64,1024]{1,0:T(8,128)S(1)} %copy-done), channel_id=1, source_target_pairs={{0,4},{2,6},{4,0},{6,2},{1,5},{3,7},{5,1},{7,3},{8,12},{10,14},{12... | collective-permute-start | bytes 786440 | tf_op jit(solution)/shard_map/ppermute | solution.py:16
  15.6 11.4 %collective-permute-start.2 = (f32[64,1024]{1,0:T(8,128)S(1)}, f32[64,1024]{1,0:T(8,128)S(1)}, u32[]{:S(2)}, u32[]{:S(2)}) collective-permute-start(f32[64,1024]{1,0:T(8,128)S(1)} %copy-done), channel_id=1, source_target_pairs={{0,6},{2,0},{4,2},{6,4},{1,7},{3,1},{5,3},{7,5},{8,14},{10,8},{12,... | collective-permute-start | bytes 786440 | tf_op jit(solution)/shard_map/ppermute | solution.py:16
  17.1 10.5 %collective-permute-start.3 = (f32[64,1024]{1,0:T(8,128)S(1)}, f32[64,1024]{1,0:T(8,128)S(1)}, u32[]{:S(2)}, u32[]{:S(2)}) collective-permute-start(f32[64,1024]{1,0:T(8,128)S(1)} %copy-done), channel_id=1, source_target_pairs={{0,1},{1,0},{2,3},{3,2},{4,5},{5,4},{6,7},{7,6},{8,9},{9,8},{10,11... | collective-permute-start | bytes 786440 | tf_op jit(solution)/shard_map/ppermute | solution.py:20
  20.9 6.7 %collective-permute-start.4 = (f32[64,1024]{1,0:T(8,128)S(1)}, f32[64,1024]{1,0:T(8,128)S(1)}, u32[]{:S(2)}, u32[]{:S(2)}) collective-permute-start(f32[64,1024]{1,0:T(8,128)S(1)} %collective-permute-done.refs_1_), channel_id=1, source_target_pairs={{0,1},{1,0},{2,3},{3,2},{4,5},{5,4},{6,7},{7,6},{8,9},{9,8},{10,11... | collective-permute-start | bytes 786440 | tf_op jit(solution)/shard_map/ppermute | solution.py:20
  31.8 9.2 %collective-permute-start.7 = (f32[512,128]{1,0:T(8,128)S(1)}, f32[512,128]{1,0:T(8,128)S(1)}, u32[]{:S(2)}, u32[]{:S(2)}) collective-permute-start(f32[512,128]{1,0:T(8,128)S(1)} %get-tuple-element.15.refs_0_), channel_id=1, source_target_pairs={{0,64},{64,128},{128,192},{192,0},{1,65},{65,129},{129,193},{193,1... | collective-permute-start | bytes 786440 | tf_op jit(solution)/shard_map/ppermute | solution.py:16
  33.5 10.7 %collective-permute-start.8 = (f32[512,128]{1,0:T(8,128)S(1)}, f32[512,128]{1,0:T(8,128)S(1)}, u32[]{:S(2)}, u32[]{:S(2)}) collective-permute-start(f32[512,128]{1,0:T(8,128)S(1)} %get-tuple-element.15.refs_0_), channel_id=1, source_target_pairs={{0,128},{64,192},{128,0},{192,64},{1,129},{65,193},{129,1},{193,65... | collective-permute-start | bytes 786440 | tf_op jit(solution)/shard_map/ppermute | solution.py:16
  34.4 13.6 %collective-permute-start.9 = (f32[512,128]{1,0:T(8,128)S(1)}, f32[512,128]{1,0:T(8,128)S(1)}, u32[]{:S(2)}, u32[]{:S(2)}) collective-permute-start(f32[512,128]{1,0:T(8,128)S(1)} %get-tuple-element.15.refs_0_), channel_id=1, source_target_pairs={{0,192},{64,0},{128,64},{192,128},{1,193},{65,1},{129,65},{193,129... | collective-permute-start | bytes 786440 | tf_op jit(solution)/shard_map/ppermute | solution.py:16
  50.7 58.1 %all-to-all-start.1 = ((f32[8,64,1024]{2,1,0:T(8,128)}), f32[8,64,1024]{2,1,0:T(8,128)}, u32[]{:S(2)}, u32[]{:S(2)}) async-start(f32[8,64,1024]{2,1,0:T(8,128)} %shard_map.69.refs_5_), calls=%async_computation.1 | async-start | bytes 4194304 | tf_op jit(solution)/shard_map/all_to_all | solution.py:253
  59.2 5.7 %collective-permute-start.10 = (f32[4,64,512]{2,1,0:T(8,128)S(1)}, f32[4,64,512]{2,1,0:T(8,128)S(1)}, u32[]{:S(2)}, u32[]{:S(2)}) collective-permute-start(f32[4,64,512]{2,1,0:T(8,128)S(1)} %get-tuple-element.18), channel_id=1, source_target_pairs={{0,1},{1,0},{2,3},{3,2},{4,5},{5,4},{6,7},{7,6},{8,9},{9,8},{10,11... | collective-permute-start | bytes 1572872 | tf_op jit(solution)/shard_map/ppermute | solution.py:20
  59.9 15.8 %collective-permute-start.15 = (f32[8,16,512]{2,1,0:T(8,128)S(1)}, f32[8,16,512]{2,1,0:T(8,128)S(1)}, u32[]{:S(2)}, u32[]{:S(2)}) collective-permute-start(f32[8,16,512]{2,1,0:T(8,128)S(1)} %shard_map.72.refs_0_), channel_id=1, source_target_pairs={{0,2},{2,4},{4,6},{6,0},{1,3},{3,5},{5,7},{7,1},{8,10},{10,12},{12... | collective-permute-start | bytes 786440 | tf_op jit(solution)/shard_map/ppermute | solution.py:16
  60.9 15.1 %collective-permute-start.16 = (f32[8,16,512]{2,1,0:T(8,128)S(1)}, f32[8,16,512]{2,1,0:T(8,128)S(1)}, u32[]{:S(2)}, u32[]{:S(2)}) collective-permute-start(f32[8,16,512]{2,1,0:T(8,128)S(1)} %shard_map.72.refs_0_), channel_id=1, source_target_pairs={{0,4},{2,6},{4,0},{6,2},{1,5},{3,7},{5,1},{7,3},{8,12},{10,14},{12... | collective-permute-start | bytes 786440 | tf_op jit(solution)/shard_map/ppermute | solution.py:16
  63.3 13.5 %collective-permute-start.17 = (f32[8,16,512]{2,1,0:T(8,128)S(1)}, f32[8,16,512]{2,1,0:T(8,128)S(1)}, u32[]{:S(2)}, u32[]{:S(2)}) collective-permute-start(f32[8,16,512]{2,1,0:T(8,128)S(1)} %shard_map.72.refs_0_), channel_id=1, source_target_pairs={{0,6},{2,0},{4,2},{6,4},{1,7},{3,1},{5,3},{7,5},{8,14},{10,8},{12,... | collective-permute-start | bytes 786440 | tf_op jit(solution)/shard_map/ppermute | solution.py:16
  65.5 13.1 %collective-permute-start.13 = (f32[64,512]{1,0:T(8,128)S(1)}, f32[64,512]{1,0:T(8,128)S(1)}, u32[]{:S(2)}, u32[]{:S(2)}) collective-permute-start(f32[64,512]{1,0:T(8,128)S(1)} %get-tuple-element.22), channel_id=1, source_target_pairs={{0,2},{2,4},{4,6},{6,0},{1,3},{3,5},{5,7},{7,1},{8,10},{10,12},{12... | collective-permute-start | bytes 393224 | tf_op jit(solution)/shard_map/ppermute | solution.py:16
  66.0 15.2 %collective-permute-start.12 = (f32[64,512]{1,0:T(8,128)S(1)}, f32[64,512]{1,0:T(8,128)S(1)}, u32[]{:S(2)}, u32[]{:S(2)}) collective-permute-start(f32[64,512]{1,0:T(8,128)S(1)} %get-tuple-element.21), channel_id=1, source_target_pairs={{0,4},{2,6},{4,0},{6,2},{1,5},{3,7},{5,1},{7,3},{8,12},{10,14},{12... | collective-permute-start | bytes 393224 | tf_op jit(solution)/shard_map/ppermute | solution.py:16
  75.7 6.0 %collective-permute-start.11 = (f32[64,512]{1,0:T(8,128)S(1)}, f32[64,512]{1,0:T(8,128)S(1)}, u32[]{:S(2)}, u32[]{:S(2)}) collective-permute-start(f32[64,512]{1,0:T(8,128)S(1)} %get-tuple-element.20), channel_id=1, source_target_pairs={{0,6},{2,0},{4,2},{6,4},{1,7},{3,1},{5,3},{7,5},{8,14},{10,8},{12,... | collective-permute-start | bytes 393224 | tf_op jit(solution)/shard_map/ppermute | solution.py:16
  76.0 6.7 %collective-permute-start.18 = (f32[8,16,512]{2,1,0:T(8,128)S(1)}, f32[8,16,512]{2,1,0:T(8,128)S(1)}, u32[]{:S(2)}, u32[]{:S(2)}) collective-permute-start(f32[8,16,512]{2,1,0:T(8,128)S(1)} %shard_map.72.refs_0_), channel_id=1, source_target_pairs={{0,1},{1,0},{2,3},{3,2},{4,5},{5,4},{6,7},{7,6},{8,9},{9,8},{10,11... | collective-permute-start | bytes 786440 | tf_op jit(solution)/shard_map/ppermute | solution.py:20
  76.8 5.9 %collective-permute-start.19 = (f32[8,16,512]{2,1,0:T(8,128)S(1)}, f32[8,16,512]{2,1,0:T(8,128)S(1)}, u32[]{:S(2)}, u32[]{:S(2)}) collective-permute-start(f32[8,16,512]{2,1,0:T(8,128)S(1)} %collective-permute-done.15.refs_1_), channel_id=1, source_target_pairs={{0,1},{1,0},{2,3},{3,2},{4,5},{5,4},{6,7},{7,6},{8,9},{9,8},{10,11... | collective-permute-start | bytes 786440 | tf_op jit(solution)/shard_map/ppermute | solution.py:20
  88.5 7.5 %collective-permute-start.22 = (f32[64,512]{1,0:T(8,128)S(1)}, f32[64,512]{1,0:T(8,128)S(1)}, u32[]{:S(2)}, u32[]{:S(2)}) collective-permute-start(f32[64,512]{1,0:T(8,128)S(1)} %shard_map.74.refs_0_.refs_4_), channel_id=1, source_target_pairs={{0,2},{2,4},{4,6},{6,0},{1,3},{3,5},{5,7},{7,1},{8,10},{10,12},{12... | collective-permute-start | bytes 393224 | tf_op jit(solution)/shard_map/ppermute | solution.py:16
  90.3 7.8 %collective-permute-start.23 = (f32[64,512]{1,0:T(8,128)S(1)}, f32[64,512]{1,0:T(8,128)S(1)}, u32[]{:S(2)}, u32[]{:S(2)}) collective-permute-start(f32[64,512]{1,0:T(8,128)S(1)} %shard_map.74.refs_0_.refs_4_), channel_id=1, source_target_pairs={{0,4},{2,6},{4,0},{6,2},{1,5},{3,7},{5,1},{7,3},{8,12},{10,14},{12... | collective-permute-start | bytes 393224 | tf_op jit(solution)/shard_map/ppermute | solution.py:16
  100.9 6.0 %collective-permute-start.29 = (f32[256,128]{1,0:T(8,128)S(1)}, f32[256,128]{1,0:T(8,128)S(1)}, u32[]{:S(2)}, u32[]{:S(2)}) collective-permute-start(f32[256,128]{1,0:T(8,128)S(1)} %shard_map.75.own), channel_id=1, source_target_pairs={{0,64},{64,0},{128,192},{192,128},{1,65},{65,1},{129,193},{193,129... | collective-permute-start | bytes 393224 | tf_op jit(solution)/shard_map/ppermute | solution.py:20
  108.8 41.3 %all-to-all-start.2 = ((f32[8,80,512]{2,1,0:T(8,128)}), f32[8,80,512]{2,1,0:T(8,128)S(1)}, u32[]{:S(2)}, u32[]{:S(2)}) async-start(f32[8,80,512]{2,1,0:T(8,128)} %shard_map.77), calls=%async_computation.2 | async-start | bytes 2621440 | tf_op jit(solution)/shard_map/all_to_all | solution.py:283
  117.0 13.4 %collective-permute-start.30 = (f32[16,1024]{0,1:T(8,128)}, f32[16,1024]{0,1:T(8,128)}, u32[]{:S(2)}, u32[]{:S(2)}) collective-permute-start(f32[16,1024]{0,1:T(8,128)} %dynamic-slice_bitcast_fusion), channel_id=1, source_target_pairs={{0,64},{64,0},{128,192},{192,128},{1,65},{65,1},{129,193},{193,129... | collective-permute-start | bytes 196616 | tf_op jit(solution)/shard_map/ppermute | solution.py:20
  (14 other events, 49.4 us)

commit v4 on v3

--- a/solution.py
+++ b/solution.py
@@ -43,7 +43,7 @@
 COLS = ((0,), (0,))
 
 
-def call(body, outs, scratch=(), n_in=1, aliases=None, in_specs=None, out_specs=None, grid=(), copies=0):
+def call(body, outs, scratch=(), n_in=1, aliases=None, in_specs=None, out_specs=None, grid=(), copies=0, weight=0):
     vmem = pl.BlockSpec(memory_space=pltpu.VMEM)
     smem = pl.BlockSpec(memory_space=pltpu.SMEM)
     return pl.pallas_call(
@@ -55,6 +55,7 @@
         scratch_shapes=[pltpu.VMEM(shape, F32) for shape in scratch]
         + ([pltpu.SemaphoreType.DMA((copies,))] if copies else []),
         input_output_aliases=aliases or {},
+        cost_estimate=pl.CostEstimate(flops=weight, transcendentals=0, bytes_accessed=0) if weight else None,
         compiler_params=pltpu.CompilerParams(vmem_limit_bytes=48 * 2**20),
     )
 
@@ -249,6 +250,7 @@
         out_specs=[outside],
         aliases={NY // 2 + 2: 0},
         copies=NZ // 2,
+        weight=17_000_000_000,
     )(at, *columns[NY // 2:], whole, root)[0]
     summed = lax.all_to_all(root, "z", 0, 0, tiled=True)
 
@@ -265,7 +267,7 @@
 
     node_all = call(whole_node, [(NZ, NXC, node_rows, width)], n_in=NXC)(at, *nodes)[0]
     node_all = node_all.reshape(NZ * NXC * node_rows, width)
-    solved = call(solve, [(rows, width)], n_in=3)(at, mixed, from_partner(mixed, "y"), node_all)[0]
+    solved = call(solve, [(rows, width)], n_in=3, weight=25_000_000_000)(at, mixed, from_partner(mixed, "y"), node_all)[0]
     solved = chip_blocks(solved)
 
     own = call(choose, [(NX * rows, 2 * width // NXC)], [(NXC * rows, width)], NXC)(at, *solved)[0]

time: 153 us -> 150 us (0.980)
  starting transfers between devices: 48.4 us -> 41.7 us
  waiting for transfers between devices: 73.9 us -> 76.2 us
    ppermute x15, waiting for transfers between devices: 38 us -> 27.8 us  [shifted(): lax.ppermute(value, axis, [(i, (i + step) % size) for i in range(size)])]
    all_to_all x1, waiting for transfers between devices: 0.01 us -> 9.04 us  [on_device(): stacks = lax.all_to_all(stacks, 'z', 0, 0, tiled=True)]
    all_to_all x1, starting transfers between devices: 7.2 us -> 3.57 us  [on_device(): both = lax.all_to_all(both, 'z', 0, 0, tiled=True)]
    all_to_all x1, waiting for transfers between devices: 0.01 us -> 2.56 us  [on_device(): summed = lax.all_to_all(root, 'z', 0, 0, tiled=True)]
    all_to_all x1, starting transfers between devices: 6.86 us -> 4.34 us  [on_device(): summed = lax.all_to_all(root, 'z', 0, 0, tiled=True)]
  transfers between devices with their start and end apart: 34 -> 34, of which waited for: 23 -> 24; matrix products, arithmetic and copies ran while one was open for 4% -> 5% of each run, Pallas kernels for 11% -> 11%
where the time goes in v4:
time: 150 us; the launch traced here: 148 us
  waiting for transfers between devices  76.2 us (51%)
  starting transfers between devices  41.7 us (28%)
  Pallas kernels  20 us (13%)
  local copies, waits for them, and re-layouts  3.94 us (3%)
  other arithmetic  3.5 us (2%)
  matrix products  2.22 us (1%)
    ppermute x15, waiting for transfers between devices, shifted(): lax.ppermute(value, axis, [(i, (i + step) % size) for i in range(size)])  27.8 us
    ppermute x16, waiting for transfers between devices, from_partner(): lax.ppermute(value, axis, [(i, i ^ 1) for i in range(lax.axis_size(axis))])  21.7 us
    ppermute x15, starting transfers between devices, shifted(): lax.ppermute(value, axis, [(i, (i + step) % size) for i in range(size)])  21.5 us
    all_to_all x1, waiting for transfers between devices, on_device(): both = lax.all_to_all(both, 'z', 0, 0, tiled=True)  15 us
    all_to_all x1, waiting for transfers between devices, on_device(): stacks = lax.all_to_all(stacks, 'z', 0, 0, tiled=True)  9.04 us
    all_to_all x1, starting transfers between devices, on_device(): stacks = lax.all_to_all(stacks, 'z', 0, 0, tiled=True)  8.47 us
    all_to_all x1, starting transfers between devices, on_device(): summed = lax.all_to_all(root, 'z', 0, 0, tiled=True)  4.34 us
    ppermute x16, starting transfers between devices, from_partner(): lax.ppermute(value, axis, [(i, i ^ 1) for i in range(lax.axis_size(axis))])  3.84 us
  transfers between devices with their start and end apart: 34, of which 24 were waited for; matrix products, arithmetic and copies ran while one was open for 5% of the time, Pallas kernels for 11%

profile of v4, /device:TPU:8, one launch (start us, length us, event | category | flops | bytes accessed | tf_op | source)
XLA Modules:
  0.0 148.3 jit_solution(7280689440367525883)
XLA Ops:
  2.2 2.7 %collective-permute-start.1 = (f32[64,1024]{1,0:T(8,128)}, f32[64,1024]{1,0:T(8,128)S(1)}, u32[]{:S(2)}, u32[]{:S(2)}) collective-permute-start(f32[64,1024]{1,0:T(8,128)} %refs_0_.1), channel_id=1, source_target_pairs={{0,4},{2,6},{4,0},{6,2},{1,5},{3,7},{5,1},{7,3},{8,12},{10,14},{12... | collective-permute-start | bytes 786440 | tf_op jit(solution)/shard_map/ppermute | solution.py:16
  8.6 8.5 %all-to-all-start = ((f32[8,80,512]{2,1,0:T(8,128)}), f32[8,80,512]{2,1,0:T(8,128)S(1)}, u32[]{:S(2)}, u32[]{:S(2)}) async-start(f32[8,80,512]{2,1,0:T(8,128)} %broadcast_in_dim.2), calls=%async_computation | async-start | bytes 2621440 | tf_op jit(solution)/shard_map/all_to_all | solution.py:233
  25.3 2.4 %collective-permute-start.9 = (f32[512,128]{1,0:T(8,128)S(1)}, f32[512,128]{1,0:T(8,128)S(1)}, u32[]{:S(2)}, u32[]{:S(2)}) collective-permute-start(f32[512,128]{1,0:T(8,128)S(1)} %get-tuple-element.15.refs_0_), channel_id=1, source_target_pairs={{0,192},{64,0},{128,64},{192,128},{1,193},{65,1},{129,65},{193,129... | collective-permute-start | bytes 786440 | tf_op jit(solution)/shard_map/ppermute | solution.py:16
  27.7 4.2 %collective-permute-done.7.refs_1_ = f32[512,128]{1,0:T(8,128)S(1)} collective-permute-done((f32[512,128]{1,0:T(8,128)S(1)}, f32[512,128]{1,0:T(8,128)S(1)}, u32[]{:S(2)}, u32[]{:S(2)}) %collective-permute-start.7) | collective-permute-done | bytes 262176 | tf_op jit(solution)/shard_map/ppermute | solution.py:16
  31.9 2.7 %shard_map.68.refs_3_ = f32[8,64,1024]{2,1,0:T(8,128)} custom-call(s32[4]{0:T(128)S(1)} %pad_add_fusion.at, f32[512,128]{1,0:T(8,128)S(1)} %get-tuple-element.15.refs_0_, f32[512,128]{1,0:T(8,128)S(1)} %collective-permute-done.7.refs_1_, f32[512,1024]{1,0:T(8,128)S(1)} %get-tuple-element.16.refs_2_), custom_call_target="tpu_custom_call" | custom-call | tf_op jit(solution)/shard_map/pallas_call | solution.py:242
  35.1 3.8 %collective-permute-done.9.refs_1_.refs_3_ = f32[512,128]{1,0:T(8,128)S(1)} collective-permute-done((f32[512,128]{1,0:T(8,128)S(1)}, f32[512,128]{1,0:T(8,128)S(1)}, u32[]{:S(2)}, u32[]{:S(2)}) %collective-permute-start.9) | collective-permute-done | bytes 262176 | tf_op jit(solution)/shard_map/ppermute | solution.py:16
  38.9 2.6 %shard_map.69.refs_5_ = f32[8,64,1024]{2,1,0:T(8,128)} custom-call(s32[4]{0:T(128)S(1)} %pad_add_fusion.at, f32[512,128]{1,0:T(8,128)S(1)} %collective-permute-done.8.refs_0_.refs_2_, f32[512,128]{1,0:T(8,128)S(1)} %collective-permute-done.9.refs_1_.refs_3_, f32[512,1024]{1,0:T(8,128)S(1)} %get-tuple-element.16.refs_2_, ...), custom_call_target="tpu_custom_call", output_to_operand_aliasing={{}: (4, {})} | custom-call | flops 16999999488 | tf_op jit(solution)/shard_map/pallas_call | solution.py:245
  41.5 9.0 %all-to-all-done.refs_4_.stacks = f32[8,80,512]{2,1,0:T(8,128)S(1)} async-done(((f32[8,80,512]{2,1,0:T(8,128)}), f32[8,80,512]{2,1,0:T(8,128)S(1)}, u32[]{:S(2)}, u32[]{:S(2)}) %all-to-all-start) | async-done | bytes 1310752 | tf_op jit(solution)/shard_map/all_to_all | solution.py:233
  50.6 2.4 %shard_map.70 = (f32[4,64,512]{2,1,0:T(8,128)S(1)}, f32[4,64,512]{2,1,0:T(8,128)}) custom-call(s32[4]{0:T(128)S(1)} %pad_add_fusion.at, s32[2,32]{1,0:T(2,128)S(1)} %copy-done.3, f32[512,128]{1,0:T(8,128)S(1)} %get-tuple-element.15.refs_0_, f32[512,128]{1,0:T(8,128)S(1)} %collective-permute-done.7.refs_1_, ...), custom_call_target="tpu_custom_call" | custom-call | tf_op jit(solution)/shard_map/pallas_call | solution.py:257
  53.0 4.3 %all-to-all-start.1 = ((f32[8,64,1024]{2,1,0:T(8,128)}), f32[8,64,1024]{2,1,0:T(8,128)}, u32[]{:S(2)}, u32[]{:S(2)}) async-start(f32[8,64,1024]{2,1,0:T(8,128)} %shard_map.69.refs_5_), calls=%async_computation.1 | async-start | bytes 4194304 | tf_op jit(solution)/shard_map/all_to_all | solution.py:255
  65.5 8.4 %collective-permute-done.15.refs_1_ = f32[8,16,512]{2,1,0:T(8,128)S(1)} collective-permute-done((f32[8,16,512]{2,1,0:T(8,128)S(1)}, f32[8,16,512]{2,1,0:T(8,128)S(1)}, u32[]{:S(2)}, u32[]{:S(2)}) %collective-permute-start.15) | collective-permute-done | bytes 262176 | tf_op jit(solution)/shard_map/ppermute | solution.py:16
  74.9 4.3 %collective-permute-done.13 = f32[64,512]{1,0:T(8,128)S(1)} collective-permute-done((f32[64,512]{1,0:T(8,128)S(1)}, f32[64,512]{1,0:T(8,128)S(1)}, u32[]{:S(2)}, u32[]{:S(2)}) %collective-permute-start.13) | collective-permute-done | bytes 131104 | tf_op jit(solution)/shard_map/ppermute | solution.py:16
  82.0 3.2 %collective-permute-done.14.other = f32[64,512]{1,0:T(8,128)S(1)} collective-permute-done((f32[64,512]{1,0:T(8,128)S(1)}, f32[64,512]{1,0:T(8,128)S(1)}, u32[]{:S(2)}, u32[]{:S(2)}) %collective-permute-start.14) | collective-permute-done | bytes 131104 | tf_op jit(solution)/shard_map/ppermute | solution.py:20
  87.2 3.6 %collective-permute-start.23 = (f32[64,512]{1,0:T(8,128)S(1)}, f32[64,512]{1,0:T(8,128)S(1)}, u32[]{:S(2)}, u32[]{:S(2)}) collective-permute-start(f32[64,512]{1,0:T(8,128)S(1)} %shard_map.74.refs_0_.refs_4_), channel_id=1, source_target_pairs={{0,4},{2,6},{4,0},{6,2},{1,5},{3,7},{5,1},{7,3},{8,12},{10,14},{12... | collective-permute-start | bytes 393224 | tf_op jit(solution)/shard_map/ppermute | solution.py:16
  90.8 2.9 %collective-permute-done.22.refs_1_.refs_5_ = f32[64,512]{1,0:T(8,128)S(1)} collective-permute-done((f32[64,512]{1,0:T(8,128)S(1)}, f32[64,512]{1,0:T(8,128)S(1)}, u32[]{:S(2)}, u32[]{:S(2)}) %collective-permute-start.22) | collective-permute-done | bytes 131104 | tf_op jit(solution)/shard_map/ppermute | solution.py:16
  93.8 2.6 %collective-permute-done.23.refs_2_.refs_6_ = f32[64,512]{1,0:T(8,128)S(1)} collective-permute-done((f32[64,512]{1,0:T(8,128)S(1)}, f32[64,512]{1,0:T(8,128)S(1)}, u32[]{:S(2)}, u32[]{:S(2)}) %collective-permute-start.23) | collective-permute-done | bytes 131104 | tf_op jit(solution)/shard_map/ppermute | solution.py:16
  99.9 2.7 %shard_map.76.refs_8_ = f32[8,80,512]{2,1,0:T(8,128)} custom-call(s32[4]{0:T(128)S(1)} %pad_add_fusion.at, f32[512,128]{1,0:T(8,128)S(1)} %get-tuple-element.15.refs_0_, f32[512,128]{1,0:T(8,128)S(1)} %collective-permute-done.7.refs_1_, f32[512,128]{1,0:T(8,128)S(1)} %collective-permute-done.8.refs_0_.refs_2_, ...), custom_call_target="tpu_custom_call" | custom-call | tf_op jit(solution)/shard_map/pallas_call | solution.py:274
  102.6 2.6 %collective-permute-done.29.other = f32[256,128]{1,0:T(8,128)S(1)} collective-permute-done((f32[256,128]{1,0:T(8,128)S(1)}, f32[256,128]{1,0:T(8,128)S(1)}, u32[]{:S(2)}, u32[]{:S(2)}) %collective-permute-start.29) | collective-permute-done | bytes 131104 | tf_op jit(solution)/shard_map/ppermute | solution.py:20
  107.0 2.6 %all-to-all-done.1 = f32[8,64,1024]{2,1,0:T(8,128)} async-done(((f32[8,64,1024]{2,1,0:T(8,128)}), f32[8,64,1024]{2,1,0:T(8,128)}, u32[]{:S(2)}, u32[]{:S(2)}) %all-to-all-start.1) | async-done | bytes 2097184 | tf_op jit(solution)/shard_map/all_to_all | solution.py:255
  109.5 3.6 %all-to-all-start.2 = ((f32[8,80,512]{2,1,0:T(8,128)}), f32[8,80,512]{2,1,0:T(8,128)S(1)}, u32[]{:S(2)}, u32[]{:S(2)}) async-start(f32[8,80,512]{2,1,0:T(8,128)} %shard_map.77), calls=%async_computation.2 | async-start | bytes 2621440 | tf_op jit(solution)/shard_map/all_to_all | solution.py:285
  114.6 12.7 %collective-permute-done.30 = f32[16,1024]{0,1:T(8,128)} collective-permute-done((f32[16,1024]{0,1:T(8,128)}, f32[16,1024]{0,1:T(8,128)}, u32[]{:S(2)}, u32[]{:S(2)}) %collective-permute-start.30) | collective-permute-done | bytes 65568 | tf_op jit(solution)/shard_map/ppermute | solution.py:20
  127.3 2.2 %fusion.gram = f32[16,512]{1,0:T(8,128)S(1)} fusion(f32[1024,512]{1,0:T(8,128)S(1)} %bitcast.10, f32[16,1024]{0,1:T(8,128)} %dynamic-slice_bitcast_fusion, f32[16,1024]{0,1:T(8,128)} %collective-permute-done.30, pred[]{:T(512)S(6)} %eq.6), kind=kOutput, calls=%fused_computation | convolution fusion | flops 100679680 | bytes 2260993 | tf_op jit(solution)/shard_map/dot_general | solution.py:290
  129.6 2.5 %reduce_sum.9 = f32[64,1024]{1,0:T(8,128)} reduce(f32[8,64,1024]{2,1,0:T(8,128)} %all-to-all-done.1, f32[]{:T(128)} %constant.49.clone.1), dimensions={0}, to_apply=%region_0.1 | reduce | flops 458752 | bytes 2359300 | tf_op jit(solution)/shard_map/reduce_sum | solution.py:294
  132.0 15.0 %all-to-all-done.2.got = f32[8,80,512]{2,1,0:T(8,128)S(1)} async-done(((f32[8,80,512]{2,1,0:T(8,128)}), f32[8,80,512]{2,1,0:T(8,128)S(1)}, u32[]{:S(2)}, u32[]{:S(2)}) %all-to-all-start.2) | async-done | bytes 1310752 | tf_op jit(solution)/shard_map/all_to_all | solution.py:285
  (71 shorter events, 35.9 us)
Async XLA Ops:
  0.6 16.5 %collective-permute-start = (f32[64,1024]{1,0:T(8,128)}, f32[64,1024]{1,0:T(8,128)S(1)}, u32[]{:S(2)}, u32[]{:S(2)}) collective-permute-start(f32[64,1024]{1,0:T(8,128)} %refs_0_.1), channel_id=1, source_target_pairs={{0,2},{2,4},{4,6},{6,0},{1,3},{3,5},{5,7},{7,1},{8,10},{10,12},{12... | collective-permute-start | bytes 786440 | tf_op jit(solution)/shard_map/ppermute | solution.py:16
  2.2 15.5 %collective-permute-start.1 = (f32[64,1024]{1,0:T(8,128)}, f32[64,1024]{1,0:T(8,128)S(1)}, u32[]{:S(2)}, u32[]{:S(2)}) collective-permute-start(f32[64,1024]{1,0:T(8,128)} %refs_0_.1), channel_id=1, source_target_pairs={{0,4},{2,6},{4,0},{6,2},{1,5},{3,7},{5,1},{7,3},{8,12},{10,14},{12... | collective-permute-start | bytes 786440 | tf_op jit(solution)/shard_map/ppermute | solution.py:16
  4.9 12.8 %collective-permute-start.2 = (f32[64,1024]{1,0:T(8,128)}, f32[64,1024]{1,0:T(8,128)S(1)}, u32[]{:S(2)}, u32[]{:S(2)}) collective-permute-start(f32[64,1024]{1,0:T(8,128)} %refs_0_.1), channel_id=1, source_target_pairs={{0,6},{2,0},{4,2},{6,4},{1,7},{3,1},{5,3},{7,5},{8,14},{10,8},{12,... | collective-permute-start | bytes 786440 | tf_op jit(solution)/shard_map/ppermute | solution.py:16
  8.6 42.0 %all-to-all-start = ((f32[8,80,512]{2,1,0:T(8,128)}), f32[8,80,512]{2,1,0:T(8,128)S(1)}, u32[]{:S(2)}, u32[]{:S(2)}) async-start(f32[8,80,512]{2,1,0:T(8,128)} %broadcast_in_dim.2), calls=%async_computation | async-start | bytes 2621440 | tf_op jit(solution)/shard_map/all_to_all | solution.py:233
  22.7 9.2 %collective-permute-start.7 = (f32[512,128]{1,0:T(8,128)S(1)}, f32[512,128]{1,0:T(8,128)S(1)}, u32[]{:S(2)}, u32[]{:S(2)}) collective-permute-start(f32[512,128]{1,0:T(8,128)S(1)} %get-tuple-element.15.refs_0_), channel_id=1, source_target_pairs={{0,64},{64,128},{128,192},{192,0},{1,65},{65,129},{129,193},{193,1... | collective-permute-start | bytes 786440 | tf_op jit(solution)/shard_map/ppermute | solution.py:16
  24.4 10.7 %collective-permute-start.8 = (f32[512,128]{1,0:T(8,128)S(1)}, f32[512,128]{1,0:T(8,128)S(1)}, u32[]{:S(2)}, u32[]{:S(2)}) collective-permute-start(f32[512,128]{1,0:T(8,128)S(1)} %get-tuple-element.15.refs_0_), channel_id=1, source_target_pairs={{0,128},{64,192},{128,0},{192,64},{1,129},{65,193},{129,1},{193,65... | collective-permute-start | bytes 786440 | tf_op jit(solution)/shard_map/ppermute | solution.py:16
  25.3 13.6 %collective-permute-start.9 = (f32[512,128]{1,0:T(8,128)S(1)}, f32[512,128]{1,0:T(8,128)S(1)}, u32[]{:S(2)}, u32[]{:S(2)}) collective-permute-start(f32[512,128]{1,0:T(8,128)S(1)} %get-tuple-element.15.refs_0_), channel_id=1, source_target_pairs={{0,192},{64,0},{128,64},{192,128},{1,193},{65,1},{129,65},{193,129... | collective-permute-start | bytes 786440 | tf_op jit(solution)/shard_map/ppermute | solution.py:16
  53.0 8.4 %collective-permute-start.10 = (f32[4,64,512]{2,1,0:T(8,128)}, f32[4,64,512]{2,1,0:T(8,128)}, u32[]{:S(2)}, u32[]{:S(2)}) collective-permute-start(f32[4,64,512]{2,1,0:T(8,128)} %get-tuple-element.18), channel_id=1, source_target_pairs={{0,1},{1,0},{2,3},{3,2},{4,5},{5,4},{6,7},{7,6},{8,9},{9,8},{10,11... | collective-permute-start | bytes 1572872 | tf_op jit(solution)/shard_map/ppermute | solution.py:20
  53.0 56.5 %all-to-all-start.1 = ((f32[8,64,1024]{2,1,0:T(8,128)}), f32[8,64,1024]{2,1,0:T(8,128)}, u32[]{:S(2)}, u32[]{:S(2)}) async-start(f32[8,64,1024]{2,1,0:T(8,128)} %shard_map.69.refs_5_), calls=%async_computation.1 | async-start | bytes 4194304 | tf_op jit(solution)/shard_map/all_to_all | solution.py:255
  58.0 16.0 %collective-permute-start.15 = (f32[8,16,512]{2,1,0:T(8,128)S(1)}, f32[8,16,512]{2,1,0:T(8,128)S(1)}, u32[]{:S(2)}, u32[]{:S(2)}) collective-permute-start(f32[8,16,512]{2,1,0:T(8,128)S(1)} %shard_map.72.refs_0_), channel_id=1, source_target_pairs={{0,2},{2,4},{4,6},{6,0},{1,3},{3,5},{5,7},{7,1},{8,10},{10,12},{12... | collective-permute-start | bytes 786440 | tf_op jit(solution)/shard_map/ppermute | solution.py:16
  58.6 15.4 %collective-permute-start.16 = (f32[8,16,512]{2,1,0:T(8,128)S(1)}, f32[8,16,512]{2,1,0:T(8,128)S(1)}, u32[]{:S(2)}, u32[]{:S(2)}) collective-permute-start(f32[8,16,512]{2,1,0:T(8,128)S(1)} %shard_map.72.refs_0_), channel_id=1, source_target_pairs={{0,4},{2,6},{4,0},{6,2},{1,5},{3,7},{5,1},{7,3},{8,12},{10,14},{12... | collective-permute-start | bytes 786440 | tf_op jit(solution)/shard_map/ppermute | solution.py:16
  59.8 15.1 %collective-permute-start.17 = (f32[8,16,512]{2,1,0:T(8,128)S(1)}, f32[8,16,512]{2,1,0:T(8,128)S(1)}, u32[]{:S(2)}, u32[]{:S(2)}) collective-permute-start(f32[8,16,512]{2,1,0:T(8,128)S(1)} %shard_map.72.refs_0_), channel_id=1, source_target_pairs={{0,6},{2,0},{4,2},{6,4},{1,7},{3,1},{5,3},{7,5},{8,14},{10,8},{12,... | collective-permute-start | bytes 786440 | tf_op jit(solution)/shard_map/ppermute | solution.py:16
  62.5 16.6 %collective-permute-start.13 = (f32[64,512]{1,0:T(8,128)S(1)}, f32[64,512]{1,0:T(8,128)S(1)}, u32[]{:S(2)}, u32[]{:S(2)}) collective-permute-start(f32[64,512]{1,0:T(8,128)S(1)} %get-tuple-element.22), channel_id=1, source_target_pairs={{0,2},{2,4},{4,6},{6,0},{1,3},{3,5},{5,7},{7,1},{8,10},{10,12},{12... | collective-permute-start | bytes 393224 | tf_op jit(solution)/shard_map/ppermute | solution.py:16
  63.4 15.8 %collective-permute-start.12 = (f32[64,512]{1,0:T(8,128)S(1)}, f32[64,512]{1,0:T(8,128)S(1)}, u32[]{:S(2)}, u32[]{:S(2)}) collective-permute-start(f32[64,512]{1,0:T(8,128)S(1)} %get-tuple-element.21), channel_id=1, source_target_pairs={{0,4},{2,6},{4,0},{6,2},{1,5},{3,7},{5,1},{7,3},{8,12},{10,14},{12... | collective-permute-start | bytes 393224 | tf_op jit(solution)/shard_map/ppermute | solution.py:16
  74.0 5.9 %collective-permute-start.11 = (f32[64,512]{1,0:T(8,128)S(1)}, f32[64,512]{1,0:T(8,128)S(1)}, u32[]{:S(2)}, u32[]{:S(2)}) collective-permute-start(f32[64,512]{1,0:T(8,128)S(1)} %get-tuple-element.20), channel_id=1, source_target_pairs={{0,6},{2,0},{4,2},{6,4},{1,7},{3,1},{5,3},{7,5},{8,14},{10,8},{12,... | collective-permute-start | bytes 393224 | tf_op jit(solution)/shard_map/ppermute | solution.py:16
  74.0 6.5 %collective-permute-start.18 = (f32[8,16,512]{2,1,0:T(8,128)S(1)}, f32[8,16,512]{2,1,0:T(8,128)S(1)}, u32[]{:S(2)}, u32[]{:S(2)}) collective-permute-start(f32[8,16,512]{2,1,0:T(8,128)S(1)} %shard_map.72.refs_0_), channel_id=1, source_target_pairs={{0,1},{1,0},{2,3},{3,2},{4,5},{5,4},{6,7},{7,6},{8,9},{9,8},{10,11... | collective-permute-start | bytes 786440 | tf_op jit(solution)/shard_map/ppermute | solution.py:20
  74.9 5.5 %collective-permute-start.19 = (f32[8,16,512]{2,1,0:T(8,128)S(1)}, f32[8,16,512]{2,1,0:T(8,128)S(1)}, u32[]{:S(2)}, u32[]{:S(2)}) collective-permute-start(f32[8,16,512]{2,1,0:T(8,128)S(1)} %collective-permute-done.15.refs_1_), channel_id=1, source_target_pairs={{0,1},{1,0},{2,3},{3,2},{4,5},{5,4},{6,7},{7,6},{8,9},{9,8},{10,11... | collective-permute-start | bytes 786440 | tf_op jit(solution)/shard_map/ppermute | solution.py:20
  86.5 7.2 %collective-permute-start.22 = (f32[64,512]{1,0:T(8,128)S(1)}, f32[64,512]{1,0:T(8,128)S(1)}, u32[]{:S(2)}, u32[]{:S(2)}) collective-permute-start(f32[64,512]{1,0:T(8,128)S(1)} %shard_map.74.refs_0_.refs_4_), channel_id=1, source_target_pairs={{0,2},{2,4},{4,6},{6,0},{1,3},{3,5},{5,7},{7,1},{8,10},{10,12},{12... | collective-permute-start | bytes 393224 | tf_op jit(solution)/shard_map/ppermute | solution.py:16
  87.2 9.1 %collective-permute-start.23 = (f32[64,512]{1,0:T(8,128)S(1)}, f32[64,512]{1,0:T(8,128)S(1)}, u32[]{:S(2)}, u32[]{:S(2)}) collective-permute-start(f32[64,512]{1,0:T(8,128)S(1)} %shard_map.74.refs_0_.refs_4_), channel_id=1, source_target_pairs={{0,4},{2,6},{4,0},{6,2},{1,5},{3,7},{5,1},{7,3},{8,12},{10,14},{12... | collective-permute-start | bytes 393224 | tf_op jit(solution)/shard_map/ppermute | solution.py:16
  90.8 5.6 %collective-permute-start.24 = (f32[64,512]{1,0:T(8,128)S(1)}, f32[64,512]{1,0:T(8,128)S(1)}, u32[]{:S(2)}, u32[]{:S(2)}) collective-permute-start(f32[64,512]{1,0:T(8,128)S(1)} %shard_map.74.refs_0_.refs_4_), channel_id=1, source_target_pairs={{0,6},{2,0},{4,2},{6,4},{1,7},{3,1},{5,3},{7,5},{8,14},{10,8},{12,... | collective-permute-start | bytes 393224 | tf_op jit(solution)/shard_map/ppermute | solution.py:16
  90.8 6.0 %collective-permute-start.25 = (f32[64,512]{1,0:T(8,128)S(1)}, f32[64,512]{1,0:T(8,128)S(1)}, u32[]{:S(2)}, u32[]{:S(2)}) collective-permute-start(f32[64,512]{1,0:T(8,128)S(1)} %shard_map.74.refs_0_.refs_4_), channel_id=1, source_target_pairs={{0,1},{1,0},{2,3},{3,2},{4,5},{5,4},{6,7},{7,6},{8,9},{9,8},{10,11... | collective-permute-start | bytes 393224 | tf_op jit(solution)/shard_map/ppermute | solution.py:20
  99.1 6.0 %collective-permute-start.29 = (f32[256,128]{1,0:T(8,128)S(1)}, f32[256,128]{1,0:T(8,128)S(1)}, u32[]{:S(2)}, u32[]{:S(2)}) collective-permute-start(f32[256,128]{1,0:T(8,128)S(1)} %shard_map.75.own), channel_id=1, source_target_pairs={{0,64},{64,0},{128,192},{192,128},{1,65},{65,1},{129,193},{193,129... | collective-permute-start | bytes 393224 | tf_op jit(solution)/shard_map/ppermute | solution.py:20
  109.5 37.5 %all-to-all-start.2 = ((f32[8,80,512]{2,1,0:T(8,128)}), f32[8,80,512]{2,1,0:T(8,128)S(1)}, u32[]{:S(2)}, u32[]{:S(2)}) async-start(f32[8,80,512]{2,1,0:T(8,128)} %shard_map.77), calls=%async_computation.2 | async-start | bytes 2621440 | tf_op jit(solution)/shard_map/all_to_all | solution.py:285
  114.2 13.2 %collective-permute-start.30 = (f32[16,1024]{0,1:T(8,128)}, f32[16,1024]{0,1:T(8,128)}, u32[]{:S(2)}, u32[]{:S(2)}) collective-permute-start(f32[16,1024]{0,1:T(8,128)} %dynamic-slice_bitcast_fusion), channel_id=1, source_target_pairs={{0,64},{64,0},{128,192},{192,128},{1,65},{65,1},{129,193},{193,129... | collective-permute-start | bytes 196616 | tf_op jit(solution)/shard_map/ppermute | solution.py:20
  (14 other events, 49.4 us)

commit v5 on v4

--- a/solution.py
+++ b/solution.py
@@ -182,7 +182,9 @@
     src = lax.broadcasted_iota(jnp.int32, (full.shape[1], take), 0)
     dst = lax.broadcasted_iota(jnp.int32, (full.shape[1], take), 1)
     pick = src == dst // node_rows * (NXC * node_rows) + (at[2] * NC + at[3]) * node_rows + dst % node_rows
-    taken = product(full[...], jnp.where(pick, 1.0, 0.0).astype(F32), ROWS)
+    pick = jnp.where(pick, 1.0, 0.0).astype(jnp.bfloat16)
+    high, low = (lax.dot_general(part, pick, (ROWS, ((), ())), preferred_element_type=F32) for part in halves(full[...]))
+    taken = high + low
     out[...] = jnp.concatenate([taken[:size], taken[size:]], axis=1)
 
 

time: 150 us -> 150 us (level)
  no operation moved by 1% of the time
where the time goes in v5:
time: 150 us; the launch traced here: 148 us
  waiting for transfers between devices  76.2 us (51%)
  starting transfers between devices  41.7 us (28%)
  Pallas kernels  19.8 us (13%)
  local copies, waits for them, and re-layouts  3.94 us (3%)
  other arithmetic  3.5 us (2%)
  matrix products  2.22 us (1%)
    ppermute x15, waiting for transfers between devices, shifted(): lax.ppermute(value, axis, [(i, (i + step) % size) for i in range(size)])  27.8 us
    ppermute x16, waiting for transfers between devices, from_partner(): lax.ppermute(value, axis, [(i, i ^ 1) for i in range(lax.axis_size(axis))])  21.6 us
    ppermute x15, starting transfers between devices, shifted(): lax.ppermute(value, axis, [(i, (i + step) % size) for i in range(size)])  21.5 us
    all_to_all x1, waiting for transfers between devices, on_device(): both = lax.all_to_all(both, 'z', 0, 0, tiled=True)  15 us
    all_to_all x1, waiting for transfers between devices, on_device(): stacks = lax.all_to_all(stacks, 'z', 0, 0, tiled=True)  9.04 us
    all_to_all x1, starting transfers between devices, on_device(): stacks = lax.all_to_all(stacks, 'z', 0, 0, tiled=True)  8.47 us
    all_to_all x1, starting transfers between devices, on_device(): summed = lax.all_to_all(root, 'z', 0, 0, tiled=True)  4.34 us
    ppermute x16, starting transfers between devices, from_partner(): lax.ppermute(value, axis, [(i, i ^ 1) for i in range(lax.axis_size(axis))])  3.84 us
  transfers between devices with their start and end apart: 34, of which 24 were waited for; matrix products, arithmetic and copies ran while one was open for 5% of the time, Pallas kernels for 11%

profile of v5, /device:TPU:8, one launch (start us, length us, event | category | flops | bytes accessed | tf_op | source)
XLA Modules:
  0.0 148.1 jit_solution(13952556974977678137)
XLA Ops:
  2.2 2.7 %collective-permute-start.1 = (f32[64,1024]{1,0:T(8,128)}, f32[64,1024]{1,0:T(8,128)S(1)}, u32[]{:S(2)}, u32[]{:S(2)}) collective-permute-start(f32[64,1024]{1,0:T(8,128)} %refs_0_.1), channel_id=1, source_target_pairs={{0,4},{2,6},{4,0},{6,2},{1,5},{3,7},{5,1},{7,3},{8,12},{10,14},{12... | collective-permute-start | bytes 786440 | tf_op jit(solution)/shard_map/ppermute | solution.py:16
  8.6 8.5 %all-to-all-start = ((f32[8,80,512]{2,1,0:T(8,128)}), f32[8,80,512]{2,1,0:T(8,128)S(1)}, u32[]{:S(2)}, u32[]{:S(2)}) async-start(f32[8,80,512]{2,1,0:T(8,128)} %broadcast_in_dim.2), calls=%async_computation | async-start | bytes 2621440 | tf_op jit(solution)/shard_map/all_to_all | solution.py:235
  25.3 2.4 %collective-permute-start.9 = (f32[512,128]{1,0:T(8,128)S(1)}, f32[512,128]{1,0:T(8,128)S(1)}, u32[]{:S(2)}, u32[]{:S(2)}) collective-permute-start(f32[512,128]{1,0:T(8,128)S(1)} %get-tuple-element.15.refs_0_), channel_id=1, source_target_pairs={{0,192},{64,0},{128,64},{192,128},{1,193},{65,1},{129,65},{193,129... | collective-permute-start | bytes 786440 | tf_op jit(solution)/shard_map/ppermute | solution.py:16
  27.7 4.2 %collective-permute-done.7.refs_1_ = f32[512,128]{1,0:T(8,128)S(1)} collective-permute-done((f32[512,128]{1,0:T(8,128)S(1)}, f32[512,128]{1,0:T(8,128)S(1)}, u32[]{:S(2)}, u32[]{:S(2)}) %collective-permute-start.7) | collective-permute-done | bytes 262176 | tf_op jit(solution)/shard_map/ppermute | solution.py:16
  31.9 2.7 %shard_map.68.refs_3_ = f32[8,64,1024]{2,1,0:T(8,128)} custom-call(s32[4]{0:T(128)S(1)} %pad_add_fusion.at, f32[512,128]{1,0:T(8,128)S(1)} %get-tuple-element.15.refs_0_, f32[512,128]{1,0:T(8,128)S(1)} %collective-permute-done.7.refs_1_, f32[512,1024]{1,0:T(8,128)S(1)} %get-tuple-element.16.refs_2_), custom_call_target="tpu_custom_call" | custom-call | tf_op jit(solution)/shard_map/pallas_call | solution.py:244
  35.1 3.8 %collective-permute-done.9.refs_1_.refs_3_ = f32[512,128]{1,0:T(8,128)S(1)} collective-permute-done((f32[512,128]{1,0:T(8,128)S(1)}, f32[512,128]{1,0:T(8,128)S(1)}, u32[]{:S(2)}, u32[]{:S(2)}) %collective-permute-start.9) | collective-permute-done | bytes 262176 | tf_op jit(solution)/shard_map/ppermute | solution.py:16
  38.9 2.6 %shard_map.69.refs_5_ = f32[8,64,1024]{2,1,0:T(8,128)} custom-call(s32[4]{0:T(128)S(1)} %pad_add_fusion.at, f32[512,128]{1,0:T(8,128)S(1)} %collective-permute-done.8.refs_0_.refs_2_, f32[512,128]{1,0:T(8,128)S(1)} %collective-permute-done.9.refs_1_.refs_3_, f32[512,1024]{1,0:T(8,128)S(1)} %get-tuple-element.16.refs_2_, ...), custom_call_target="tpu_custom_call", output_to_operand_aliasing={{}: (4, {})} | custom-call | flops 16999999488 | tf_op jit(solution)/shard_map/pallas_call | solution.py:247
  41.5 9.0 %all-to-all-done.refs_4_.stacks = f32[8,80,512]{2,1,0:T(8,128)S(1)} async-done(((f32[8,80,512]{2,1,0:T(8,128)}), f32[8,80,512]{2,1,0:T(8,128)S(1)}, u32[]{:S(2)}, u32[]{:S(2)}) %all-to-all-start) | async-done | bytes 1310752 | tf_op jit(solution)/shard_map/all_to_all | solution.py:235
  50.6 2.4 %shard_map.70 = (f32[4,64,512]{2,1,0:T(8,128)S(1)}, f32[4,64,512]{2,1,0:T(8,128)}) custom-call(s32[4]{0:T(128)S(1)} %pad_add_fusion.at, s32[2,32]{1,0:T(2,128)S(1)} %copy-done.3, f32[512,128]{1,0:T(8,128)S(1)} %get-tuple-element.15.refs_0_, f32[512,128]{1,0:T(8,128)S(1)} %collective-permute-done.7.refs_1_, ...), custom_call_target="tpu_custom_call" | custom-call | tf_op jit(solution)/shard_map/pallas_call | solution.py:259
  53.0 4.3 %all-to-all-start.1 = ((f32[8,64,1024]{2,1,0:T(8,128)}), f32[8,64,1024]{2,1,0:T(8,128)}, u32[]{:S(2)}, u32[]{:S(2)}) async-start(f32[8,64,1024]{2,1,0:T(8,128)} %shard_map.69.refs_5_), calls=%async_computation.1 | async-start | bytes 4194304 | tf_op jit(solution)/shard_map/all_to_all | solution.py:257
  65.5 8.4 %collective-permute-done.15.refs_1_ = f32[8,16,512]{2,1,0:T(8,128)S(1)} collective-permute-done((f32[8,16,512]{2,1,0:T(8,128)S(1)}, f32[8,16,512]{2,1,0:T(8,128)S(1)}, u32[]{:S(2)}, u32[]{:S(2)}) %collective-permute-start.15) | collective-permute-done | bytes 262176 | tf_op jit(solution)/shard_map/ppermute | solution.py:16
  74.9 4.3 %collective-permute-done.13 = f32[64,512]{1,0:T(8,128)S(1)} collective-permute-done((f32[64,512]{1,0:T(8,128)S(1)}, f32[64,512]{1,0:T(8,128)S(1)}, u32[]{:S(2)}, u32[]{:S(2)}) %collective-permute-start.13) | collective-permute-done | bytes 131104 | tf_op jit(solution)/shard_map/ppermute | solution.py:16
  82.0 3.2 %collective-permute-done.14.other = f32[64,512]{1,0:T(8,128)S(1)} collective-permute-done((f32[64,512]{1,0:T(8,128)S(1)}, f32[64,512]{1,0:T(8,128)S(1)}, u32[]{:S(2)}, u32[]{:S(2)}) %collective-permute-start.14) | collective-permute-done | bytes 131104 | tf_op jit(solution)/shard_map/ppermute | solution.py:20
  87.2 3.6 %collective-permute-start.23 = (f32[64,512]{1,0:T(8,128)S(1)}, f32[64,512]{1,0:T(8,128)S(1)}, u32[]{:S(2)}, u32[]{:S(2)}) collective-permute-start(f32[64,512]{1,0:T(8,128)S(1)} %shard_map.74.refs_0_.refs_4_), channel_id=1, source_target_pairs={{0,4},{2,6},{4,0},{6,2},{1,5},{3,7},{5,1},{7,3},{8,12},{10,14},{12... | collective-permute-start | bytes 393224 | tf_op jit(solution)/shard_map/ppermute | solution.py:16
  90.8 2.9 %collective-permute-done.22.refs_1_.refs_5_ = f32[64,512]{1,0:T(8,128)S(1)} collective-permute-done((f32[64,512]{1,0:T(8,128)S(1)}, f32[64,512]{1,0:T(8,128)S(1)}, u32[]{:S(2)}, u32[]{:S(2)}) %collective-permute-start.22) | collective-permute-done | bytes 131104 | tf_op jit(solution)/shard_map/ppermute | solution.py:16
  93.8 2.6 %collective-permute-done.23.refs_2_.refs_6_ = f32[64,512]{1,0:T(8,128)S(1)} collective-permute-done((f32[64,512]{1,0:T(8,128)S(1)}, f32[64,512]{1,0:T(8,128)S(1)}, u32[]{:S(2)}, u32[]{:S(2)}) %collective-permute-start.23) | collective-permute-done | bytes 131104 | tf_op jit(solution)/shard_map/ppermute | solution.py:16
  99.7 2.7 %shard_map.76.refs_8_ = f32[8,80,512]{2,1,0:T(8,128)} custom-call(s32[4]{0:T(128)S(1)} %pad_add_fusion.at, f32[512,128]{1,0:T(8,128)S(1)} %get-tuple-element.15.refs_0_, f32[512,128]{1,0:T(8,128)S(1)} %collective-permute-done.7.refs_1_, f32[512,128]{1,0:T(8,128)S(1)} %collective-permute-done.8.refs_0_.refs_2_, ...), custom_call_target="tpu_custom_call" | custom-call | tf_op jit(solution)/shard_map/pallas_call | solution.py:276
  102.5 2.6 %collective-permute-done.29.other = f32[256,128]{1,0:T(8,128)S(1)} collective-permute-done((f32[256,128]{1,0:T(8,128)S(1)}, f32[256,128]{1,0:T(8,128)S(1)}, u32[]{:S(2)}, u32[]{:S(2)}) %collective-permute-start.29) | collective-permute-done | bytes 131104 | tf_op jit(solution)/shard_map/ppermute | solution.py:20
  106.8 2.7 %all-to-all-done.1 = f32[8,64,1024]{2,1,0:T(8,128)} async-done(((f32[8,64,1024]{2,1,0:T(8,128)}), f32[8,64,1024]{2,1,0:T(8,128)}, u32[]{:S(2)}, u32[]{:S(2)}) %all-to-all-start.1) | async-done | bytes 2097184 | tf_op jit(solution)/shard_map/all_to_all | solution.py:257
  109.5 3.6 %all-to-all-start.2 = ((f32[8,80,512]{2,1,0:T(8,128)}), f32[8,80,512]{2,1,0:T(8,128)S(1)}, u32[]{:S(2)}, u32[]{:S(2)}) async-start(f32[8,80,512]{2,1,0:T(8,128)} %shard_map.77), calls=%async_computation.2 | async-start | bytes 2621440 | tf_op jit(solution)/shard_map/all_to_all | solution.py:287
  114.6 12.6 %collective-permute-done.30 = f32[16,1024]{0,1:T(8,128)} collective-permute-done((f32[16,1024]{0,1:T(8,128)}, f32[16,1024]{0,1:T(8,128)}, u32[]{:S(2)}, u32[]{:S(2)}) %collective-permute-start.30) | collective-permute-done | bytes 65568 | tf_op jit(solution)/shard_map/ppermute | solution.py:20
  127.2 2.2 %fusion.gram = f32[16,512]{1,0:T(8,128)S(1)} fusion(f32[1024,512]{1,0:T(8,128)S(1)} %bitcast.10, f32[16,1024]{0,1:T(8,128)} %dynamic-slice_bitcast_fusion, f32[16,1024]{0,1:T(8,128)} %collective-permute-done.30, pred[]{:T(512)S(6)} %eq.6), kind=kOutput, calls=%fused_computation | convolution fusion | flops 100679680 | bytes 2260993 | tf_op jit(solution)/shard_map/dot_general | solution.py:292
  129.4 2.5 %reduce_sum.9 = f32[64,1024]{1,0:T(8,128)} reduce(f32[8,64,1024]{2,1,0:T(8,128)} %all-to-all-done.1, f32[]{:T(128)} %constant.49.clone.1), dimensions={0}, to_apply=%region_0.1 | reduce | flops 458752 | bytes 2359300 | tf_op jit(solution)/shard_map/reduce_sum | solution.py:296
  131.8 15.0 %all-to-all-done.2.got = f32[8,80,512]{2,1,0:T(8,128)S(1)} async-done(((f32[8,80,512]{2,1,0:T(8,128)}), f32[8,80,512]{2,1,0:T(8,128)S(1)}, u32[]{:S(2)}, u32[]{:S(2)}) %all-to-all-start.2) | async-done | bytes 1310752 | tf_op jit(solution)/shard_map/all_to_all | solution.py:287
  (71 shorter events, 35.7 us)
Async XLA Ops:
  0.6 16.5 %collective-permute-start = (f32[64,1024]{1,0:T(8,128)}, f32[64,1024]{1,0:T(8,128)S(1)}, u32[]{:S(2)}, u32[]{:S(2)}) collective-permute-start(f32[64,1024]{1,0:T(8,128)} %refs_0_.1), channel_id=1, source_target_pairs={{0,2},{2,4},{4,6},{6,0},{1,3},{3,5},{5,7},{7,1},{8,10},{10,12},{12... | collective-permute-start | bytes 786440 | tf_op jit(solution)/shard_map/ppermute | solution.py:16
  2.2 15.5 %collective-permute-start.1 = (f32[64,1024]{1,0:T(8,128)}, f32[64,1024]{1,0:T(8,128)S(1)}, u32[]{:S(2)}, u32[]{:S(2)}) collective-permute-start(f32[64,1024]{1,0:T(8,128)} %refs_0_.1), channel_id=1, source_target_pairs={{0,4},{2,6},{4,0},{6,2},{1,5},{3,7},{5,1},{7,3},{8,12},{10,14},{12... | collective-permute-start | bytes 786440 | tf_op jit(solution)/shard_map/ppermute | solution.py:16
  4.9 12.8 %collective-permute-start.2 = (f32[64,1024]{1,0:T(8,128)}, f32[64,1024]{1,0:T(8,128)S(1)}, u32[]{:S(2)}, u32[]{:S(2)}) collective-permute-start(f32[64,1024]{1,0:T(8,128)} %refs_0_.1), channel_id=1, source_target_pairs={{0,6},{2,0},{4,2},{6,4},{1,7},{3,1},{5,3},{7,5},{8,14},{10,8},{12,... | collective-permute-start | bytes 786440 | tf_op jit(solution)/shard_map/ppermute | solution.py:16
  8.6 42.0 %all-to-all-start = ((f32[8,80,512]{2,1,0:T(8,128)}), f32[8,80,512]{2,1,0:T(8,128)S(1)}, u32[]{:S(2)}, u32[]{:S(2)}) async-start(f32[8,80,512]{2,1,0:T(8,128)} %broadcast_in_dim.2), calls=%async_computation | async-start | bytes 2621440 | tf_op jit(solution)/shard_map/all_to_all | solution.py:235
  22.7 9.2 %collective-permute-start.7 = (f32[512,128]{1,0:T(8,128)S(1)}, f32[512,128]{1,0:T(8,128)S(1)}, u32[]{:S(2)}, u32[]{:S(2)}) collective-permute-start(f32[512,128]{1,0:T(8,128)S(1)} %get-tuple-element.15.refs_0_), channel_id=1, source_target_pairs={{0,64},{64,128},{128,192},{192,0},{1,65},{65,129},{129,193},{193,1... | collective-permute-start | bytes 786440 | tf_op jit(solution)/shard_map/ppermute | solution.py:16
  24.4 10.7 %collective-permute-start.8 = (f32[512,128]{1,0:T(8,128)S(1)}, f32[512,128]{1,0:T(8,128)S(1)}, u32[]{:S(2)}, u32[]{:S(2)}) collective-permute-start(f32[512,128]{1,0:T(8,128)S(1)} %get-tuple-element.15.refs_0_), channel_id=1, source_target_pairs={{0,128},{64,192},{128,0},{192,64},{1,129},{65,193},{129,1},{193,65... | collective-permute-start | bytes 786440 | tf_op jit(solution)/shard_map/ppermute | solution.py:16
  25.3 13.6 %collective-permute-start.9 = (f32[512,128]{1,0:T(8,128)S(1)}, f32[512,128]{1,0:T(8,128)S(1)}, u32[]{:S(2)}, u32[]{:S(2)}) collective-permute-start(f32[512,128]{1,0:T(8,128)S(1)} %get-tuple-element.15.refs_0_), channel_id=1, source_target_pairs={{0,192},{64,0},{128,64},{192,128},{1,193},{65,1},{129,65},{193,129... | collective-permute-start | bytes 786440 | tf_op jit(solution)/shard_map/ppermute | solution.py:16
  53.0 8.4 %collective-permute-start.10 = (f32[4,64,512]{2,1,0:T(8,128)}, f32[4,64,512]{2,1,0:T(8,128)}, u32[]{:S(2)}, u32[]{:S(2)}) collective-permute-start(f32[4,64,512]{2,1,0:T(8,128)} %get-tuple-element.18), channel_id=1, source_target_pairs={{0,1},{1,0},{2,3},{3,2},{4,5},{5,4},{6,7},{7,6},{8,9},{9,8},{10,11... | collective-permute-start | bytes 1572872 | tf_op jit(solution)/shard_map/ppermute | solution.py:20
  53.0 56.5 %all-to-all-start.1 = ((f32[8,64,1024]{2,1,0:T(8,128)}), f32[8,64,1024]{2,1,0:T(8,128)}, u32[]{:S(2)}, u32[]{:S(2)}) async-start(f32[8,64,1024]{2,1,0:T(8,128)} %shard_map.69.refs_5_), calls=%async_computation.1 | async-start | bytes 4194304 | tf_op jit(solution)/shard_map/all_to_all | solution.py:257
  58.0 16.0 %collective-permute-start.15 = (f32[8,16,512]{2,1,0:T(8,128)S(1)}, f32[8,16,512]{2,1,0:T(8,128)S(1)}, u32[]{:S(2)}, u32[]{:S(2)}) collective-permute-start(f32[8,16,512]{2,1,0:T(8,128)S(1)} %shard_map.72.refs_0_), channel_id=1, source_target_pairs={{0,2},{2,4},{4,6},{6,0},{1,3},{3,5},{5,7},{7,1},{8,10},{10,12},{12... | collective-permute-start | bytes 786440 | tf_op jit(solution)/shard_map/ppermute | solution.py:16
  58.6 15.4 %collective-permute-start.16 = (f32[8,16,512]{2,1,0:T(8,128)S(1)}, f32[8,16,512]{2,1,0:T(8,128)S(1)}, u32[]{:S(2)}, u32[]{:S(2)}) collective-permute-start(f32[8,16,512]{2,1,0:T(8,128)S(1)} %shard_map.72.refs_0_), channel_id=1, source_target_pairs={{0,4},{2,6},{4,0},{6,2},{1,5},{3,7},{5,1},{7,3},{8,12},{10,14},{12... | collective-permute-start | bytes 786440 | tf_op jit(solution)/shard_map/ppermute | solution.py:16
  59.8 15.1 %collective-permute-start.17 = (f32[8,16,512]{2,1,0:T(8,128)S(1)}, f32[8,16,512]{2,1,0:T(8,128)S(1)}, u32[]{:S(2)}, u32[]{:S(2)}) collective-permute-start(f32[8,16,512]{2,1,0:T(8,128)S(1)} %shard_map.72.refs_0_), channel_id=1, source_target_pairs={{0,6},{2,0},{4,2},{6,4},{1,7},{3,1},{5,3},{7,5},{8,14},{10,8},{12,... | collective-permute-start | bytes 786440 | tf_op jit(solution)/shard_map/ppermute | solution.py:16
  62.5 16.6 %collective-permute-start.13 = (f32[64,512]{1,0:T(8,128)S(1)}, f32[64,512]{1,0:T(8,128)S(1)}, u32[]{:S(2)}, u32[]{:S(2)}) collective-permute-start(f32[64,512]{1,0:T(8,128)S(1)} %get-tuple-element.22), channel_id=1, source_target_pairs={{0,2},{2,4},{4,6},{6,0},{1,3},{3,5},{5,7},{7,1},{8,10},{10,12},{12... | collective-permute-start | bytes 393224 | tf_op jit(solution)/shard_map/ppermute | solution.py:16
  63.4 15.8 %collective-permute-start.12 = (f32[64,512]{1,0:T(8,128)S(1)}, f32[64,512]{1,0:T(8,128)S(1)}, u32[]{:S(2)}, u32[]{:S(2)}) collective-permute-start(f32[64,512]{1,0:T(8,128)S(1)} %get-tuple-element.21), channel_id=1, source_target_pairs={{0,4},{2,6},{4,0},{6,2},{1,5},{3,7},{5,1},{7,3},{8,12},{10,14},{12... | collective-permute-start | bytes 393224 | tf_op jit(solution)/shard_map/ppermute | solution.py:16
  74.0 5.9 %collective-permute-start.11 = (f32[64,512]{1,0:T(8,128)S(1)}, f32[64,512]{1,0:T(8,128)S(1)}, u32[]{:S(2)}, u32[]{:S(2)}) collective-permute-start(f32[64,512]{1,0:T(8,128)S(1)} %get-tuple-element.20), channel_id=1, source_target_pairs={{0,6},{2,0},{4,2},{6,4},{1,7},{3,1},{5,3},{7,5},{8,14},{10,8},{12,... | collective-permute-start | bytes 393224 | tf_op jit(solution)/shard_map/ppermute | solution.py:16
  74.0 6.5 %collective-permute-start.18 = (f32[8,16,512]{2,1,0:T(8,128)S(1)}, f32[8,16,512]{2,1,0:T(8,128)S(1)}, u32[]{:S(2)}, u32[]{:S(2)}) collective-permute-start(f32[8,16,512]{2,1,0:T(8,128)S(1)} %shard_map.72.refs_0_), channel_id=1, source_target_pairs={{0,1},{1,0},{2,3},{3,2},{4,5},{5,4},{6,7},{7,6},{8,9},{9,8},{10,11... | collective-permute-start | bytes 786440 | tf_op jit(solution)/shard_map/ppermute | solution.py:20
  74.9 5.5 %collective-permute-start.19 = (f32[8,16,512]{2,1,0:T(8,128)S(1)}, f32[8,16,512]{2,1,0:T(8,128)S(1)}, u32[]{:S(2)}, u32[]{:S(2)}) collective-permute-start(f32[8,16,512]{2,1,0:T(8,128)S(1)} %collective-permute-done.15.refs_1_), channel_id=1, source_target_pairs={{0,1},{1,0},{2,3},{3,2},{4,5},{5,4},{6,7},{7,6},{8,9},{9,8},{10,11... | collective-permute-start | bytes 786440 | tf_op jit(solution)/shard_map/ppermute | solution.py:20
  86.5 7.2 %collective-permute-start.22 = (f32[64,512]{1,0:T(8,128)S(1)}, f32[64,512]{1,0:T(8,128)S(1)}, u32[]{:S(2)}, u32[]{:S(2)}) collective-permute-start(f32[64,512]{1,0:T(8,128)S(1)} %shard_map.74.refs_0_.refs_4_), channel_id=1, source_target_pairs={{0,2},{2,4},{4,6},{6,0},{1,3},{3,5},{5,7},{7,1},{8,10},{10,12},{12... | collective-permute-start | bytes 393224 | tf_op jit(solution)/shard_map/ppermute | solution.py:16
  87.2 9.1 %collective-permute-start.23 = (f32[64,512]{1,0:T(8,128)S(1)}, f32[64,512]{1,0:T(8,128)S(1)}, u32[]{:S(2)}, u32[]{:S(2)}) collective-permute-start(f32[64,512]{1,0:T(8,128)S(1)} %shard_map.74.refs_0_.refs_4_), channel_id=1, source_target_pairs={{0,4},{2,6},{4,0},{6,2},{1,5},{3,7},{5,1},{7,3},{8,12},{10,14},{12... | collective-permute-start | bytes 393224 | tf_op jit(solution)/shard_map/ppermute | solution.py:16
  90.8 5.6 %collective-permute-start.24 = (f32[64,512]{1,0:T(8,128)S(1)}, f32[64,512]{1,0:T(8,128)S(1)}, u32[]{:S(2)}, u32[]{:S(2)}) collective-permute-start(f32[64,512]{1,0:T(8,128)S(1)} %shard_map.74.refs_0_.refs_4_), channel_id=1, source_target_pairs={{0,6},{2,0},{4,2},{6,4},{1,7},{3,1},{5,3},{7,5},{8,14},{10,8},{12,... | collective-permute-start | bytes 393224 | tf_op jit(solution)/shard_map/ppermute | solution.py:16
  90.8 6.0 %collective-permute-start.25 = (f32[64,512]{1,0:T(8,128)S(1)}, f32[64,512]{1,0:T(8,128)S(1)}, u32[]{:S(2)}, u32[]{:S(2)}) collective-permute-start(f32[64,512]{1,0:T(8,128)S(1)} %shard_map.74.refs_0_.refs_4_), channel_id=1, source_target_pairs={{0,1},{1,0},{2,3},{3,2},{4,5},{5,4},{6,7},{7,6},{8,9},{9,8},{10,11... | collective-permute-start | bytes 393224 | tf_op jit(solution)/shard_map/ppermute | solution.py:20
  99.0 6.0 %collective-permute-start.29 = (f32[256,128]{1,0:T(8,128)S(1)}, f32[256,128]{1,0:T(8,128)S(1)}, u32[]{:S(2)}, u32[]{:S(2)}) collective-permute-start(f32[256,128]{1,0:T(8,128)S(1)} %shard_map.75.own), channel_id=1, source_target_pairs={{0,64},{64,0},{128,192},{192,128},{1,65},{65,1},{129,193},{193,129... | collective-permute-start | bytes 393224 | tf_op jit(solution)/shard_map/ppermute | solution.py:20
  109.5 37.3 %all-to-all-start.2 = ((f32[8,80,512]{2,1,0:T(8,128)}), f32[8,80,512]{2,1,0:T(8,128)S(1)}, u32[]{:S(2)}, u32[]{:S(2)}) async-start(f32[8,80,512]{2,1,0:T(8,128)} %shard_map.77), calls=%async_computation.2 | async-start | bytes 2621440 | tf_op jit(solution)/shard_map/all_to_all | solution.py:287
  114.2 13.0 %collective-permute-start.30 = (f32[16,1024]{0,1:T(8,128)}, f32[16,1024]{0,1:T(8,128)}, u32[]{:S(2)}, u32[]{:S(2)}) collective-permute-start(f32[16,1024]{0,1:T(8,128)} %dynamic-slice_bitcast_fusion), channel_id=1, source_target_pairs={{0,64},{64,0},{128,192},{192,128},{1,65},{65,1},{129,193},{193,129... | collective-permute-start | bytes 196616 | tf_op jit(solution)/shard_map/ppermute | solution.py:20
  (14 other events, 49.4 us)
